TPU v7x, 32 devices: a whole 2x2x4 slice. The times are simulated.
32 devices in a mesh: dp: 16 (over z, y, core), tensor: 2 (over x).
Axes of the slice: x: 2, y: 2, z: 4, core: 2. Of those that a mesh axis runs over, the one named last changes fastest.
Arguments:
- tokens: bfloat16 [8192, 896], P('dp'), may hold values from -6 to 6
- out_grad: bfloat16 [8192, 896], P('dp'), may hold values from -6 to 6
- doc_lengths: int32 [16, 8], P('dp'), may hold values from 0 to 512, as said below
- q_weight: bfloat16 [896, 896], P(None, 'tensor'), may hold values from -0.1875 to 0.1875
- k_weight: bfloat16 [896, 128], P(None, 'tensor'), may hold values from -0.1875 to 0.1875
- v_weight: bfloat16 [896, 128], P(None, 'tensor'), may hold values from -0.1875 to 0.1875
- q_bias: bfloat16 [14, 64], P('tensor'), may hold values from -3 to 3
- k_bias: bfloat16 [2, 64], P('tensor'), may hold values from -3 to 3
- v_bias: bfloat16 [2, 64], P('tensor'), may hold values from -3 to 3
- o_weight: bfloat16 [896, 896], P('tensor'), may hold values from -1 to 1
- attn_gain: bfloat16 [896], replicated, may hold values from 0.099609375 to 1.8984375
- ffn_gain: bfloat16 [896], replicated, may hold values from 0.099609375 to 1.8984375
- gate_weight: bfloat16 [896, 4864], P(None, 'tensor'), may hold values from -0.1875 to 0.1875
- up_weight: bfloat16 [896, 4864], P(None, 'tensor'), may hold values from -0.1875 to 0.1875
- down_weight: bfloat16 [4864, 896], P('tensor'), may hold values from -0.078125 to 0.078125
Outputs:
- layer_out: bfloat16 [8192, 896], P('dp')
- tokens_grad: bfloat16 [8192, 896], P('dp')
- q_weight_grad: float32 [896, 896], P('dp', 'tensor')
- k_weight_grad: float32 [896, 128], P('dp', 'tensor')
- v_weight_grad: float32 [896, 128], P('dp', 'tensor')
- q_bias_grad: float32 [14, 64], P('tensor', 'dp')
- k_bias_grad: float32 [2, 64], P('tensor')
- v_bias_grad: float32 [2, 64], P('tensor', 'dp')
- o_weight_grad: float32 [896, 896], P('tensor', 'dp')
- attn_gain_grad: float32 [896], P('dp')
- ffn_gain_grad: float32 [896], P('dp')
- gate_weight_grad: float32 [896, 4864], P('dp', 'tensor')
- up_weight_grad: float32 [896, 4864], P('dp', 'tensor')
- down_weight_grad: float32 [4864, 896], P('tensor', 'dp')
Inputs may be any that keep to these rules, and one draw needn't show every extreme that they name: `doc_lengths`: each row lists the sequences of one token buffer, zeros after the last; a row's sum is at most 512, every nonzero entry is 200 or more, the first entry is nonzero, and in every draw some buffer holds one sequence of exactly 512 tokens.
All inputs are finite; a program needn't handle non-finite values.
Results may differ from a plain program's by a relative error of at most 0.024.
Values sent between devices are 32-bit elements; how exact they have to be, the bound alone decides.
No kernel may reach another device: no remote copies, remote signals or barrier semaphores. Data moves between devices by JAX's collectives and lax.ppermute only.
A program may use at most 192 MiB of HBM per device.

v0:
```python
import math

import jax
import jax.numpy as jnp
from jax import lax
from jax.sharding import PartitionSpec as P

HD = 64


norm_eps = 1e-06
rope_base = 1000000.0


def layout(lengths, row_total):
    doc_ends = jnp.cumsum(lengths)
    places = jnp.arange(row_total, dtype=jnp.int32)
    passed = (places[:, None] >= doc_ends[None, :]).astype(jnp.int32)
    segment = jnp.sum(passed, axis=1)
    begins = jnp.sum(passed * lengths[None, :], axis=1)
    alive = places < doc_ends[-1]
    return (segment, places - begins, alive)


def rotary(positions, width):
    half_width = width // 2
    inv_freq = jnp.exp(
        jnp.arange(half_width, dtype=jnp.float32) * (-2.0 * math.log(rope_base) / width)
    )
    angles = positions.astype(jnp.float32)[:, None] * inv_freq[None, :]
    return (jnp.cos(angles), jnp.sin(angles))


def rotate_pairs(heads_in, cosine, sine_table):
    half_width = heads_in.shape[-1] // 2
    front_half = heads_in[..., :half_width]
    back_half = heads_in[..., half_width:]
    cos_rows = cosine[:, None, :]
    sin_rows = sine_table[:, None, :]
    return jnp.concatenate(
        [
            front_half * cos_rows - back_half * sin_rows,
            back_half * cos_rows + front_half * sin_rows,
        ],
        axis=-1,
    )


def norm_back(inputs, factor, gain, upstream):
    gain_grad = jnp.sum(upstream * (inputs * factor), axis=0)
    scaled = upstream * gain
    input_grad = factor * scaled - inputs * factor**3 * jnp.mean(
        scaled * inputs, axis=-1, keepdims=True
    )
    return (gain_grad, input_grad)


def on_device(
    tokens,
    out_grad,
    doc_lengths,
    q_weight,
    k_weight,
    v_weight,
    q_bias,
    k_bias,
    v_bias,
    o_weight,
    attn_gain,
    ffn_gain,
    gate_weight,
    up_weight,
    down_weight,
):
    row_total = tokens.shape[0]
    local_heads = q_weight.shape[1] // HD
    local_kv = k_weight.shape[1] // HD
    group_size = local_heads // local_kv
    block_rows = min(512, row_total)
    block_count = row_total // block_rows
    score_scale = HD ** (-0.5)
    segment, positions, alive = layout(doc_lengths[0], row_total)
    cosine, sine_table = rotary(positions, HD)
    alive_rows = alive.astype(jnp.float32)[:, None]
    places = jnp.arange(row_total, dtype=jnp.int32)
    inputs = tokens.astype(jnp.float32)
    gain_one = attn_gain.astype(jnp.float32)
    gain_two = ffn_gain.astype(jnp.float32)
    factor_one = lax.rsqrt(jnp.mean(inputs * inputs, axis=-1, keepdims=True) + norm_eps)
    normed = (inputs * factor_one * gain_one).astype(jnp.bfloat16)
    query_pre = jnp.dot(normed, q_weight, preferred_element_type=jnp.float32) + q_bias.reshape(
        -1
    ).astype(jnp.float32)
    key_pre = jnp.dot(normed, k_weight, preferred_element_type=jnp.float32) + k_bias.reshape(
        -1
    ).astype(jnp.float32)
    value_rows = (
        (
            jnp.dot(normed, v_weight, preferred_element_type=jnp.float32)
            + v_bias.reshape(-1).astype(jnp.float32)
        )
        .astype(jnp.bfloat16)
        .reshape(row_total, local_kv, HD)
    )
    queries = rotate_pairs(
        query_pre.reshape(row_total, local_heads, HD), cosine, sine_table
    ).astype(jnp.bfloat16)
    key_rows = rotate_pairs(key_pre.reshape(row_total, local_kv, HD), cosine, sine_table).astype(
        jnp.bfloat16
    )
    query_blocks = queries.reshape(block_count, block_rows, local_kv, group_size, HD)
    seg_blocks = segment.reshape(block_count, block_rows)
    place_blocks = places.reshape(block_count, block_rows)

    def block_scores(query_rows, seg_rows, row_places):
        scores = (
            jnp.einsum("qkgd,skd->kgqs", query_rows, key_rows, preferred_element_type=jnp.float32)
            * score_scale
        )
        allowed = (seg_rows[:, None] == segment[None, :]) & (row_places[:, None] >= places[None, :])
        return jnp.where(allowed, scores, -1e30)

    def attend(block_args):
        query_rows, seg_rows, row_places = block_args
        scores = block_scores(query_rows, seg_rows, row_places)
        top_score = jnp.max(scores, axis=-1, keepdims=True)
        exp_scores = jnp.exp(scores - top_score)
        total_mass = jnp.sum(exp_scores, axis=-1, keepdims=True)
        attn_probs = (exp_scores / total_mass).astype(jnp.bfloat16)
        mixed_rows = jnp.einsum(
            "kgqs,skd->qkgd", attn_probs, value_rows, preferred_element_type=jnp.float32
        )
        return (mixed_rows, (top_score + jnp.log(total_mass))[..., 0])

    mixed_blocks, log_mass = lax.map(attend, (query_blocks, seg_blocks, place_blocks))
    mixed_heads = mixed_blocks.reshape(row_total, local_heads * HD).astype(jnp.bfloat16)
    attn_part = jnp.dot(mixed_heads, o_weight, preferred_element_type=jnp.float32)
    residual = inputs + lax.psum(attn_part, "tensor")
    factor_two = lax.rsqrt(jnp.mean(residual * residual, axis=-1, keepdims=True) + norm_eps)
    normed_two = (residual * factor_two * gain_two).astype(jnp.bfloat16)
    gate_act = jnp.dot(normed_two, gate_weight, preferred_element_type=jnp.float32)
    up_act = jnp.dot(normed_two, up_weight, preferred_element_type=jnp.float32)
    hidden_act = (jax.nn.silu(gate_act) * up_act).astype(jnp.bfloat16)
    ffn_part = jnp.dot(hidden_act, down_weight, preferred_element_type=jnp.float32)
    block_out = residual + lax.psum(ffn_part, "tensor")
    layer_out = jnp.where(alive[:, None], block_out, inputs).astype(jnp.bfloat16)
    upstream = out_grad.astype(jnp.float32)
    branch_grad = (upstream * alive_rows).astype(jnp.bfloat16)
    down_grad = jnp.einsum("tf,td->fd", hidden_act, branch_grad, preferred_element_type=jnp.float32)
    hidden_grad = jnp.einsum(
        "td,fd->tf", branch_grad, down_weight, preferred_element_type=jnp.float32
    )
    sigmoid_gate = jax.nn.sigmoid(gate_act)
    gate_grad_rows = (
        hidden_grad * up_act * (sigmoid_gate * (1.0 + gate_act * (1.0 - sigmoid_gate)))
    ).astype(jnp.bfloat16)
    up_grad_rows = (hidden_grad * jax.nn.silu(gate_act)).astype(jnp.bfloat16)
    gate_grad = jnp.einsum(
        "td,tf->df", normed_two, gate_grad_rows, preferred_element_type=jnp.float32
    )
    up_grad = jnp.einsum("td,tf->df", normed_two, up_grad_rows, preferred_element_type=jnp.float32)
    normed_two_grad = jnp.einsum(
        "tf,df->td", gate_grad_rows, gate_weight, preferred_element_type=jnp.float32
    ) + jnp.einsum("tf,df->td", up_grad_rows, up_weight, preferred_element_type=jnp.float32)
    normed_two_grad = lax.psum(normed_two_grad, "tensor")
    ffn_gain_grad, residual_grad = norm_back(residual, factor_two, gain_two, normed_two_grad)
    residual_grad = residual_grad + upstream * alive_rows
    residual_low = residual_grad.astype(jnp.bfloat16)
    o_grad = jnp.einsum("ta,td->ad", mixed_heads, residual_low, preferred_element_type=jnp.float32)
    mixed_grad = jnp.einsum(
        "td,ad->ta", residual_low, o_weight, preferred_element_type=jnp.float32
    ).astype(jnp.bfloat16)
    grad_blocks = mixed_grad.reshape(block_count, block_rows, local_kv, group_size, HD)

    def attend_back(carry, block_args):
        key_acc, value_acc = carry
        query_rows, seg_rows, row_places, mass_rows, grad_rows = block_args
        scores = block_scores(query_rows, seg_rows, row_places)
        attn_probs = jnp.exp(scores - mass_rows[..., None])
        value_acc = value_acc + jnp.einsum(
            "kgqs,qkgd->skd",
            attn_probs.astype(jnp.bfloat16),
            grad_rows,
            preferred_element_type=jnp.float32,
        )
        prob_grad = jnp.einsum(
            "qkgd,skd->kgqs", grad_rows, value_rows, preferred_element_type=jnp.float32
        )
        inner_sum = jnp.sum(attn_probs * prob_grad, axis=-1, keepdims=True)
        score_grad = (attn_probs * (prob_grad - inner_sum)).astype(jnp.bfloat16)
        query_grad = (
            jnp.einsum("kgqs,skd->qkgd", score_grad, key_rows, preferred_element_type=jnp.float32)
            * score_scale
        )
        key_acc = (
            key_acc
            + jnp.einsum(
                "kgqs,qkgd->skd", score_grad, query_rows, preferred_element_type=jnp.float32
            )
            * score_scale
        )
        return ((key_acc, value_acc), query_grad)

    zero_acc = jnp.zeros((row_total, local_kv, HD), jnp.float32)
    (key_acc, value_acc), query_grads = lax.scan(
        attend_back,
        (zero_acc, zero_acc),
        (query_blocks, seg_blocks, place_blocks, log_mass, grad_blocks),
    )
    query_grad_rows = (
        rotate_pairs(query_grads.reshape(row_total, local_heads, HD), cosine, -sine_table)
        .reshape(row_total, local_heads * HD)
        .astype(jnp.bfloat16)
    )
    key_grad_rows = (
        rotate_pairs(key_acc, cosine, -sine_table)
        .reshape(row_total, local_kv * HD)
        .astype(jnp.bfloat16)
    )
    value_grad_rows = value_acc.reshape(row_total, local_kv * HD).astype(jnp.bfloat16)
    q_weight_grad = jnp.einsum(
        "td,ta->da", normed, query_grad_rows, preferred_element_type=jnp.float32
    )
    k_weight_grad = jnp.einsum(
        "td,ta->da", normed, key_grad_rows, preferred_element_type=jnp.float32
    )
    v_weight_grad = jnp.einsum(
        "td,ta->da", normed, value_grad_rows, preferred_element_type=jnp.float32
    )
    q_bias_grad = jnp.sum(query_grad_rows.astype(jnp.float32), axis=0).reshape(local_heads, HD)
    k_bias_grad = jnp.sum(key_grad_rows.astype(jnp.float32), axis=0).reshape(local_kv, HD)
    v_bias_grad = jnp.sum(value_grad_rows.astype(jnp.float32), axis=0).reshape(local_kv, HD)
    k_bias_tiled = jnp.broadcast_to(k_bias_grad[None], (lax.axis_size("dp"), local_kv, HD))
    normed_grad = jnp.einsum(
        "ta,da->td", query_grad_rows, q_weight, preferred_element_type=jnp.float32
    )
    normed_grad = normed_grad + jnp.einsum(
        "ta,da->td", key_grad_rows, k_weight, preferred_element_type=jnp.float32
    )
    normed_grad = normed_grad + jnp.einsum(
        "ta,da->td", value_grad_rows, v_weight, preferred_element_type=jnp.float32
    )
    normed_grad = lax.psum(normed_grad, "tensor")
    attn_gain_grad, input_grad = norm_back(inputs, factor_one, gain_one, normed_grad)
    tokens_grad = (upstream * (1.0 - alive_rows) + residual_grad + input_grad).astype(jnp.bfloat16)
    gathered = (
        lax.psum_scatter(q_weight_grad, "dp", scatter_dimension=0, tiled=True),
        lax.psum_scatter(k_weight_grad, "dp", scatter_dimension=0, tiled=True),
        lax.psum_scatter(v_weight_grad, "dp", scatter_dimension=0, tiled=True),
        lax.psum_scatter(q_bias_grad, "dp", scatter_dimension=1, tiled=True),
        lax.psum_scatter(k_bias_tiled, "dp", scatter_dimension=0, tiled=True),
        lax.psum_scatter(v_bias_grad, "dp", scatter_dimension=1, tiled=True),
        lax.psum_scatter(o_grad, "dp", scatter_dimension=1, tiled=True),
        lax.psum_scatter(attn_gain_grad, "dp", scatter_dimension=0, tiled=True),
        lax.psum_scatter(ffn_gain_grad, "dp", scatter_dimension=0, tiled=True),
        lax.psum_scatter(gate_grad, "dp", scatter_dimension=0, tiled=True),
        lax.psum_scatter(up_grad, "dp", scatter_dimension=0, tiled=True),
        lax.psum_scatter(down_grad, "dp", scatter_dimension=1, tiled=True),
    )
    k_bias_total = gathered[4].reshape(local_kv, HD)
    return (
        layer_out,
        tokens_grad,
        gathered[0],
        gathered[1],
        gathered[2],
        gathered[3],
        k_bias_total,
        gathered[5],
        gathered[6],
        gathered[7],
        gathered[8],
        gathered[9],
        gathered[10],
        gathered[11],
    )


def solution(mesh):
    return jax.shard_map(
        on_device,
        mesh=mesh,
        in_specs=(
            P("dp", None),
            P("dp", None),
            P("dp", None),
            P(None, "tensor"),
            P(None, "tensor"),
            P(None, "tensor"),
            P("tensor", None),
            P("tensor", None),
            P("tensor", None),
            P("tensor", None),
            P(),
            P(),
            P(None, "tensor"),
            P(None, "tensor"),
            P("tensor", None),
        ),
        out_specs=(
            P("dp", None),
            P("dp", None),
            P("dp", "tensor"),
            P("dp", "tensor"),
            P("dp", "tensor"),
            P("tensor", "dp"),
            P("tensor", None),
            P("tensor", "dp"),
            P("tensor", "dp"),
            P("dp"),
            P("dp"),
            P("dp", "tensor"),
            P("dp", "tensor"),
            P("tensor", "dp"),
        ),
        check_vma=False,
    )
```

profile of v0, /device:TPU:0, one launch (start us, length us, event | category | flops | bytes accessed | tf_op | source)
XLA Modules:
  0.0 888.7 jit_solution(14195093692683187458)
XLA Ops:
  29.6 57.5 %all-reduce.16.cloned.1.call-done = f32[512,896]{1,0:T(8,128)} async-done(((f32[512,896]{1,0:T(8,128)}), f32[512,896]{1,0:T(8,128)}) %all-reduce.16.cloned.1.call-update) | async-done | bytes 1835024 | tf_op jit(solution)/shard_map/psum | solution.py:138
  90.6 7.2 fusion.93
  97.9 4.5 fusion.92
  102.5 8.8 multiply_convert_fusion
  111.3 4.7 fusion.95
  116.0 4.1 convolution_add_fusion
  121.8 7.1 fusion.94
  128.8 48.7 %all-reduce.18.cloned.1.call-done = f32[512,896]{1,0:T(8,128)} async-done(((f32[512,896]{1,0:T(8,128)}), f32[512,896]{1,0:T(8,128)}) %all-reduce.18.cloned.1.call-update) | async-done | bytes 1835024 | tf_op jit(solution)/shard_map/psum | solution.py:165
  187.0 4.3 fusion
  191.3 7.1 fusion.9
  198.4 3.4 fusion.36
  210.6 3.7 fusion.46
  216.5 8.0 fusion.49
  224.6 8.1 fusion.98
  232.7 8.0 fusion.97
  245.9 58.3 %all-reduce.20.cloned.1.call-done = (f32[512,896]{1,0:T(8,128)}, f32[512,896]{1,0:T(8,128)}) async-done(((f32[512,896]{1,0:T(8,128)}, f32[512,896]{1,0:T(8,128)}), (f32[512,896]{1,0:T(8,128)}, f32[512,896]{1,0:T(8,128)})) %all-reduce.20.cloned.1.call-update) | async-done | bytes 3670032 | tf_op jit(solution)/shard_map/psum | solution.py:145
  306.3 61.3 %all-reduce.10 = (f32[7,64]{0,1:T(8,128)S(1)}, f32[16,1,64]{2,1,0:T(1,128)S(1)}, f32[1,64]{1,0:T(1,128)S(1)}, f32[896]{0:T(1024)S(1)}, f32[896]{0:T(1024)S(1)}) all-reduce(f32[7,64]{0,1:T(8,128)S(1)} %copy.42, f32[16,1,64]{2,1,0:T(1,128)S(1)} %broadcast_in_dim.59, ...), channel_id=5, replica_groups=mesh['dp'=16,'tensor'=2] {'dp'}, use_global_device_ids=true, to_apply=%region_18.19.clone | all-reduce | flops 3328 | bytes 26624
  371.1 4.5 fusion.21
  375.6 40.9 %reduce-scatter.23.cloned.1.call-done = f32[56,64]{1,0:T(8,128)} async-done(((f32[896,64]{1,0:T(8,128)}), f32[56,64]{1,0:T(8,128)}) %reduce-scatter.23.cloned.1.call-update) | async-done | bytes 14352
  416.5 63.9 %reduce-scatter.21.cloned.1.call-done = f32[448,56]{0,1:T(8,128)} async-done(((f32[448,896]{0,1:T(8,128)}), f32[448,56]{0,1:T(8,128)}) %reduce-scatter.21.cloned.1.call-update) | async-done | bytes 100368 | tf_op jit(solution)/shard_map/reduce_scatter | solution.py:253
  480.5 64.0 %reduce-scatter.19.cloned.1.call-done = f32[56,448]{1,0:T(8,128)} async-done(((f32[896,448]{1,0:T(8,128)}), f32[56,448]{1,0:T(8,128)}) %reduce-scatter.19.cloned.1.call-update) | async-done | bytes 100368 | tf_op jit(solution)/shard_map/reduce_scatter | solution.py:247
  544.4 112.3 %reduce-scatter.31.cloned.1.call-done = f32[2432,56]{0,1:T(8,128)} async-done(((f32[2432,896]{0,1:T(8,128)}), f32[2432,56]{0,1:T(8,128)}) %reduce-scatter.31.cloned.1.call-update) | async-done | bytes 544784
  656.7 112.4 %reduce-scatter.29.cloned.1.call-done = f32[56,2432]{1,0:T(8,128)} async-done(((f32[896,2432]{1,0:T(8,128)}), f32[56,2432]{1,0:T(8,128)}) %reduce-scatter.29.cloned.1.call-update) | async-done | bytes 544784
  769.2 112.3 %reduce-scatter.27.cloned.1.call-done = f32[56,2432]{1,0:T(8,128)} async-done(((f32[896,2432]{1,0:T(8,128)}), f32[56,2432]{1,0:T(8,128)}) %reduce-scatter.27.cloned.1.call-update) | async-done | bytes 544784
  (215 shorter events, 56.8 us)
Async XLA Ops:
  7.2 17.7 %copy-start = (bf16[448,896]{1,0:T(8,128)(2,1)S(1)}, bf16[448,896]{1,0:T(8,128)(2,1)}, u32[]{:S(2)}) copy-start(bf16[448,896]{1,0:T(8,128)(2,1)} %param.24) | copy-start | bytes 2408452
  7.2 10.5 %copy-start.3 = (bf16[512,896]{1,0:T(8,128)(2,1)S(1)}, bf16[512,896]{1,0:T(8,128)(2,1)}, u32[]{:S(2)}) copy-start(bf16[512,896]{1,0:T(8,128)(2,1)} %param.15) | copy-start | bytes 2752516
  7.2 10.4 %copy-start.29 = (bf16[896,64]{0,1:T(8,128)(2,1)S(1)}, bf16[896,64]{0,1:T(8,128)(2,1)}, u32[]{:S(2)}) copy-start(bf16[896,64]{0,1:T(8,128)(2,1)} %param.20) | copy-start | bytes 344068
  7.2 79.9 %all-reduce.16.cloned.1.call-start = ((), (), s32[]{:S(2)}) async-start(), calls=%async_computation.7 | async-start | bytes 3670016 | tf_op jit(solution)/shard_map/psum | solution.py:138
  7.3 10.4 %copy-start.50 = (f32[32]{0:T(128)}, f32[32]{0:T(128)S(1)}, u32[]{:S(2)}) copy-start(f32[32]{0:T(128)S(1)} %multiply_exponential_fusion) | copy-start | bytes 388
  26.9 150.6 %all-reduce.18.cloned.1.call-start = ((), (), s32[]{:S(2)}) async-start(), calls=%async_computation.8 | async-start | bytes 3670016 | tf_op jit(solution)/shard_map/psum | solution.py:165
  90.2 7.6 slice-start.2
  90.6 7.3 copy-start.9
  90.6 11.8 %slice-start.6 = ((s8[4358144]{0:T(1024)(128)(4,1)}), s8[4194304]{0:T(1024)(128)(4,1)S(1)}, s32[]{:S(2)}) async-start(s8[4358144]{0:T(1024)(128)(4,1)} %bitcast.160), calls=%async_computation.23 | async-start | bytes 8388608
  97.9 18.1 %slice-start.4 = ((s8[4358144]{0:T(1024)(128)(4,1)}), s8[4194304]{0:T(1024)(128)(4,1)S(1)}, s32[]{:S(2)}) async-start(s8[4358144]{0:T(1024)(128)(4,1)} %bitcast.158), calls=%async_computation.21 | async-start | bytes 8388608
  102.4 13.6 %slice-start.5 = ((s8[4358144]{0:T(1024)(128)(4,1)}), s8[163840]{0:T(1024)(128)(4,1)S(1)}, s32[]{:S(2)}) async-start(s8[4358144]{0:T(1024)(128)(4,1)} %bitcast.158), calls=%async_computation.22 | async-start | bytes 327680
  120.2 184.0 %all-reduce.20.cloned.1.call-start = ((), (), s32[]{:S(2)}) async-start(), calls=%async_computation.16 | async-start | bytes 7340032 | tf_op jit(solution)/shard_map/psum | solution.py:145
  177.6 7.4 slice-start
  187.0 18.0 %copy-start.20 = (bf16[512,64]{0,1:T(8,128)(2,1)}, bf16[512,64]{0,1:T(8,128)(2,1)S(1)}, u32[]{:S(2)}) copy-start(bf16[512,64]{0,1:T(8,128)(2,1)S(1)} %get-tuple-element.123) | copy-start | bytes 196612
  206.7 168.9 %reduce-scatter.25.cloned.1.call-start = ((), (), s32[]{:S(2)}) async-start(), calls=%async_computation.12 | async-start | bytes 487424
  208.9 207.6 %reduce-scatter.23.cloned.1.call-start = ((), (), s32[]{:S(2)}) async-start(), calls=%async_computation.11 | async-start | bytes 487424
  210.5 269.9 %reduce-scatter.21.cloned.1.call-start = ((), (), s32[]{:S(2)}) async-start(), calls=%async_computation.10 | async-start | bytes 1949696 | tf_op jit(solution)/shard_map/reduce_scatter | solution.py:253
  214.3 330.2 %reduce-scatter.19.cloned.1.call-start = ((), (), s32[]{:S(2)}) async-start(), calls=%async_computation.9 | async-start | bytes 1949696 | tf_op jit(solution)/shard_map/reduce_scatter | solution.py:247
  216.4 440.3 %reduce-scatter.31.cloned.1.call-start = ((), (), s32[]{:S(2)}) async-start(), calls=%async_computation.15 | async-start | bytes 9261056
  224.5 544.6 %reduce-scatter.29.cloned.1.call-start = ((), (), s32[]{:S(2)}) async-start(), calls=%async_computation.14 | async-start | bytes 9261056
  232.7 648.8 %reduce-scatter.27.cloned.1.call-start = ((), (), s32[]{:S(2)}) async-start(), calls=%async_computation.13 | async-start | bytes 9261056
  240.7 65.6 %copy-start.45 = (f32[896]{0:T(1024)S(1)}, f32[896]{0:T(1024)}, u32[]{:S(2)}) copy-start(f32[896]{0:T(1024)} %get-tuple-element.70) | copy-start | bytes 10756
  240.8 65.6 %copy-start.52 = (f32[64]{0:T(128)S(1)}, f32[64]{0:T(128)}, u32[]{:S(2)}) copy-start(f32[64]{0:T(128)} %get-tuple-element.122) | copy-start | bytes 772
  371.1 510.3 %copy-start.1 = (bf16[448,896]{1,0:T(8,128)(2,1)S(1)}, bf16[448,896]{1,0:T(8,128)(2,1)}, u32[]{:S(2)}) copy-start(bf16[448,896]{1,0:T(8,128)(2,1)} %param.24) | copy-start | bytes 2408452
  (53 other events, 144.1 us)
Sparse Core Ops, SparseCore 0:
  27.1 59.9 all-reduce.15
  120.3 57.2 all-reduce.17
  206.8 97.2 all-reduce.19
  308.0 52.6 reduce-scatter.24
  364.7 51.8 reduce-scatter.22
  420.7 59.7 reduce-scatter.20
  484.7 59.6 reduce-scatter.18
  549.0 107.6 reduce-scatter.30
  661.3 107.7 reduce-scatter.28
  773.6 107.7 reduce-scatter.26
where the time goes:
time: 894 us; the launch traced here: 889 us
  waiting for transfers between devices  671 us (75%)
  matrix products  90.3 us (10%)
  blocking collectives  61.3 us (7%)
  other arithmetic  36.7 us (4%)
  between operations  16.8 us (2%)
  local copies, waits for them, and re-layouts  12.1 us (1%)
    unnamed x15, waiting for transfers between devices  378 us
    reduce_scatter x1, waiting for transfers between devices, on_device(): lax.psum_scatter(q_weight_grad, 'dp', scatter_dimension=0, tiled=True)  64 us
    reduce_scatter x1, waiting for transfers between devices, on_device(): lax.psum_scatter(o_grad, 'dp', scatter_dimension=1, tiled=True)  63.9 us
    unnamed x1, blocking collectives  61.3 us
    psum x1, waiting for transfers between devices, on_device(): block_out = residual + lax.psum(ffn_part, 'tensor')  58.3 us
    psum x1, waiting for transfers between devices, on_device(): residual = inputs + lax.psum(attn_part, 'tensor')  57.5 us
    psum x1, waiting for transfers between devices, on_device(): normed_two_grad = lax.psum(normed_two_grad, 'tensor')  48.7 us
  transfers between devices with their start and end apart: 10, of which 9 were waited for; matrix products, arithmetic and copies ran while one was open for 6% of the time, Pallas kernels for 0%

commit v1 on v0

v1 whole, which is shorter than its diff:
```python
import math

import jax
import jax.numpy as jnp
from jax import lax
from jax.sharding import PartitionSpec as P

HD = 64


norm_eps = 1e-06
rope_base = 1000000.0


def layout(lengths, row_total):
    doc_ends = jnp.cumsum(lengths)
    places = jnp.arange(row_total, dtype=jnp.int32)
    passed = (places[:, None] >= doc_ends[None, :]).astype(jnp.int32)
    segment = jnp.sum(passed, axis=1)
    begins = jnp.sum(passed * lengths[None, :], axis=1)
    alive = places < doc_ends[-1]
    return (segment, places - begins, alive)


def rotary(positions, width):
    half_width = width // 2
    inv_freq = jnp.exp(
        jnp.arange(half_width, dtype=jnp.float32) * (-2.0 * math.log(rope_base) / width)
    )
    angles = positions.astype(jnp.float32)[:, None] * inv_freq[None, :]
    return (jnp.cos(angles), jnp.sin(angles))


def rotate_pairs(heads_in, cosine, sine_table):
    half_width = heads_in.shape[-1] // 2
    front_half = heads_in[..., :half_width]
    back_half = heads_in[..., half_width:]
    cos_rows = cosine[:, None, :]
    sin_rows = sine_table[:, None, :]
    return jnp.concatenate(
        [
            front_half * cos_rows - back_half * sin_rows,
            back_half * cos_rows + front_half * sin_rows,
        ],
        axis=-1,
    )


def norm_back(inputs, factor, gain, upstream):
    scaled = upstream * gain
    return factor * scaled - inputs * factor**3 * jnp.mean(scaled * inputs, axis=-1, keepdims=True)


def swap_tensor(rows):
    size = lax.axis_size("tensor")
    return lax.ppermute(rows, "tensor", [(i, i ^ 1) for i in range(size)])


def swap_dp(rows, bit):
    size = lax.axis_size("dp")
    return lax.ppermute(rows, "dp", [(i, i ^ (1 << bit)) for i in range(size)])


def dest_columns(width, order):
    steps = len(order)
    blocks = 1 << steps
    block = width // blocks
    own = lax.axis_index("dp")
    places = jnp.arange(width, dtype=jnp.int32)
    spot = places // block
    flip = jnp.zeros_like(spot)
    for j, bit in enumerate(order):
        flip = flip + (((spot >> (steps - 1 - j)) & 1) << bit)
    source = (own ^ flip) * block + places % block
    chosen = (jnp.arange(width, dtype=jnp.int32)[:, None] == source[None, :]).astype(jnp.bfloat16)
    return chosen[:, : width // 2], chosen[:, width // 2 :]


def pick(rows, chosen):
    return jnp.dot(rows, chosen, preferred_element_type=jnp.float32).astype(jnp.bfloat16)


def scatter_sum(kept_rows, sent_rows, features, order):
    sent = jnp.einsum("td,tf->df", sent_rows, features, preferred_element_type=jnp.float32)
    sent = swap_dp(sent, order[0])
    total = jnp.einsum("td,tf->df", kept_rows, features, preferred_element_type=jnp.float32) + sent
    for bit in order[1:]:
        half = total.shape[0] // 2
        total = total[:half] + swap_dp(total[half:], bit)
    return total


def on_device(
    tokens,
    out_grad,
    doc_lengths,
    q_weight,
    k_weight,
    v_weight,
    q_bias,
    k_bias,
    v_bias,
    o_weight,
    attn_gain,
    ffn_gain,
    gate_weight,
    up_weight,
    down_weight,
):
    row_total, width = tokens.shape
    local_heads = q_weight.shape[1] // HD
    local_kv = k_weight.shape[1] // HD
    group_size = local_heads // local_kv
    dp_size = lax.axis_size("dp")
    dp_bits = dp_size.bit_length() - 1
    ffn_order = tuple(range(dp_bits))
    attn_order = (0,) + tuple(range(2, dp_bits)) + (1,)
    own = lax.axis_index("dp")
    score_scale = HD ** (-0.5)
    segment, positions, alive = layout(doc_lengths[0], row_total)
    cosine, sine_table = rotary(positions, HD)
    alive_rows = alive.astype(jnp.float32)[:, None]
    places = jnp.arange(row_total, dtype=jnp.int32)
    inputs = tokens.astype(jnp.float32)
    gain_one = attn_gain.astype(jnp.float32)
    gain_two = ffn_gain.astype(jnp.float32)
    factor_one = lax.rsqrt(jnp.mean(inputs * inputs, axis=-1, keepdims=True) + norm_eps)
    normed = (inputs * factor_one * gain_one).astype(jnp.bfloat16)
    qkv_weight = jnp.concatenate([q_weight, k_weight, v_weight], axis=1)
    qkv_bias = jnp.concatenate([q_bias.reshape(-1), k_bias.reshape(-1), v_bias.reshape(-1)])
    qkv = jnp.dot(normed, qkv_weight, preferred_element_type=jnp.float32) + qkv_bias.astype(jnp.float32)
    q_width = local_heads * HD
    k_width = local_kv * HD
    value_rows = qkv[:, q_width + k_width :].astype(jnp.bfloat16).reshape(row_total, local_kv, HD)
    turned = rotate_pairs(
        qkv[:, : q_width + k_width].reshape(row_total, local_heads + local_kv, HD), cosine, sine_table
    ).astype(jnp.bfloat16)
    queries = turned[:, :local_heads].reshape(row_total, local_kv, group_size, HD)
    key_rows = turned[:, local_heads:]
    allowed = (segment[:, None] == segment[None, :]) & (places[:, None] >= places[None, :])
    scores = jnp.einsum("qkgd,skd->kgqs", queries, key_rows, preferred_element_type=jnp.float32) * score_scale
    scores = jnp.where(allowed, scores, -1e30)
    top_score = jnp.max(scores, axis=-1, keepdims=True)
    exp_scores = jnp.exp(scores - top_score)
    total_mass = jnp.sum(exp_scores, axis=-1, keepdims=True)
    attn_probs = exp_scores / total_mass
    low_probs = attn_probs.astype(jnp.bfloat16)
    mixed_heads = (
        jnp.einsum("kgqs,skd->qkgd", low_probs, value_rows, preferred_element_type=jnp.float32)
        .reshape(row_total, q_width)
        .astype(jnp.bfloat16)
    )
    attn_part = jnp.dot(mixed_heads, o_weight, preferred_element_type=jnp.float32)
    residual = inputs + (attn_part + swap_tensor(attn_part))
    factor_two = lax.rsqrt(jnp.mean(residual * residual, axis=-1, keepdims=True) + norm_eps)
    normed_two = (residual * factor_two * gain_two).astype(jnp.bfloat16)
    gate_act = jnp.dot(normed_two, gate_weight, preferred_element_type=jnp.float32)
    up_act = jnp.dot(normed_two, up_weight, preferred_element_type=jnp.float32)
    hidden_act = (jax.nn.silu(gate_act) * up_act).astype(jnp.bfloat16)
    upstream = out_grad.astype(jnp.float32)
    branch_grad = (upstream * alive_rows).astype(jnp.bfloat16)
    ffn_keep, ffn_send = dest_columns(width, ffn_order)
    attn_keep, attn_send = dest_columns(width, attn_order)
    down_grad = scatter_sum(pick(branch_grad, ffn_keep), pick(branch_grad, ffn_send), hidden_act, ffn_order)
    hidden_grad = jnp.einsum("td,fd->tf", branch_grad, down_weight, preferred_element_type=jnp.float32)
    sigmoid_gate = jax.nn.sigmoid(gate_act)
    gate_grad_rows = (
        hidden_grad * up_act * (sigmoid_gate * (1.0 + gate_act * (1.0 - sigmoid_gate)))
    ).astype(jnp.bfloat16)
    up_grad_rows = (hidden_grad * jax.nn.silu(gate_act)).astype(jnp.bfloat16)
    normed_two_part = jnp.einsum(
        "tf,df->td", gate_grad_rows, gate_weight, preferred_element_type=jnp.float32
    ) + jnp.einsum("tf,df->td", up_grad_rows, up_weight, preferred_element_type=jnp.float32)
    two_keep, two_send = pick(normed_two, ffn_keep), pick(normed_two, ffn_send)
    gate_grad = scatter_sum(two_keep, two_send, gate_grad_rows, ffn_order)
    up_grad = scatter_sum(two_keep, two_send, up_grad_rows, ffn_order)
    normed_two_grad = normed_two_part + swap_tensor(normed_two_part)
    ffn_gain_part = jnp.sum(normed_two_part * (residual * factor_two), axis=0)
    residual_grad = norm_back(residual, factor_two, gain_two, normed_two_grad)
    residual_grad = residual_grad + upstream * alive_rows
    residual_low = residual_grad.astype(jnp.bfloat16)
    o_grad = scatter_sum(pick(residual_low, attn_keep), pick(residual_low, attn_send), mixed_heads, attn_order)
    mixed_grad = (
        jnp.einsum("td,ad->ta", residual_low, o_weight, preferred_element_type=jnp.float32)
        .astype(jnp.bfloat16)
        .reshape(row_total, local_kv, group_size, HD)
    )
    value_acc = jnp.einsum("kgqs,qkgd->skd", low_probs, mixed_grad, preferred_element_type=jnp.float32)
    prob_grad = jnp.einsum("qkgd,skd->kgqs", mixed_grad, value_rows, preferred_element_type=jnp.float32)
    inner_sum = jnp.sum(attn_probs * prob_grad, axis=-1, keepdims=True)
    score_grad = (attn_probs * (prob_grad - inner_sum)).astype(jnp.bfloat16)
    query_acc = (
        jnp.einsum("kgqs,skd->qkgd", score_grad, key_rows, preferred_element_type=jnp.float32) * score_scale
    )
    key_acc = jnp.einsum("kgqs,qkgd->skd", score_grad, queries, preferred_element_type=jnp.float32) * score_scale
    turned_back = rotate_pairs(
        jnp.concatenate([query_acc.reshape(row_total, local_heads, HD), key_acc], axis=1), cosine, -sine_table
    )
    qkv_grad_rows = (
        jnp.concatenate([turned_back, value_acc], axis=1)
        .reshape(row_total, q_width + 2 * k_width)
        .astype(jnp.bfloat16)
    )
    normed_part = jnp.einsum("ta,da->td", qkv_grad_rows, qkv_weight, preferred_element_type=jnp.float32)
    qkv_grad = scatter_sum(pick(normed, attn_keep), pick(normed, attn_send), qkv_grad_rows, attn_order)
    attn_gain_part = jnp.sum(normed_part * (inputs * factor_one), axis=0)
    bias_part = jnp.sum(qkv_grad_rows.astype(jnp.float32), axis=0)
    normed_grad = normed_part + swap_tensor(normed_part)
    input_grad = norm_back(inputs, factor_one, gain_one, normed_grad)
    tokens_grad = (upstream * (1.0 - alive_rows) + residual_grad + input_grad).astype(jnp.bfloat16)
    gain_parts = jnp.concatenate([attn_gain_part, ffn_gain_part])
    gain_parts = gain_parts + swap_tensor(gain_parts)
    small = jnp.concatenate([gain_parts, bias_part])
    for bit in range(dp_bits):
        small = small + swap_dp(small, bit)
    gain_block = width // dp_size
    attn_gain_grad = lax.dynamic_slice_in_dim(small, own * gain_block, gain_block)
    ffn_gain_grad = lax.dynamic_slice_in_dim(small, width + own * gain_block, gain_block)
    bias_heads = small[2 * width :].reshape(local_heads + 2 * local_kv, HD)
    bias_block = HD // dp_size
    bias_own = lax.dynamic_slice_in_dim(bias_heads, own * bias_block, bias_block, axis=1)
    ffn_part = jnp.dot(hidden_act, down_weight, preferred_element_type=jnp.float32)
    block_out = residual + (ffn_part + swap_tensor(ffn_part))
    layer_out = jnp.where(alive[:, None], block_out, inputs).astype(jnp.bfloat16)
    return (
        layer_out,
        tokens_grad,
        qkv_grad[:, :q_width],
        qkv_grad[:, q_width : q_width + k_width],
        qkv_grad[:, q_width + k_width :],
        bias_own[:local_heads],
        bias_heads[local_heads : local_heads + local_kv],
        bias_own[local_heads + local_kv :],
        o_grad.T,
        attn_gain_grad,
        ffn_gain_grad,
        gate_grad,
        up_grad,
        down_grad.T,
    )


def solution(mesh):
    return jax.shard_map(
        on_device,
        mesh=mesh,
        in_specs=(
            P("dp", None),
            P("dp", None),
            P("dp", None),
            P(None, "tensor"),
            P(None, "tensor"),
            P(None, "tensor"),
            P("tensor", None),
            P("tensor", None),
            P("tensor", None),
            P("tensor", None),
            P(),
            P(),
            P(None, "tensor"),
            P(None, "tensor"),
            P("tensor", None),
        ),
        out_specs=(
            P("dp", None),
            P("dp", None),
            P("dp", "tensor"),
            P("dp", "tensor"),
            P("dp", "tensor"),
            P("tensor", "dp"),
            P("tensor", None),
            P("tensor", "dp"),
            P("tensor", "dp"),
            P("dp"),
            P("dp"),
            P("dp", "tensor"),
            P("dp", "tensor"),
            P("tensor", "dp"),
        ),
        check_vma=False,
    )
```

time: 894 us -> 507 us (0.57)
  waiting for transfers between devices: 671 us -> 298 us
  blocking collectives: 61.3 us -> 0 us
  starting transfers between devices: 1.05 us -> 37.2 us
  between operations: 16.8 us -> 1.89 us
  other arithmetic: 36.7 us -> 45.9 us
    unnamed x15 -> x0, waiting for transfers between devices: 378 us -> none
    ppermute x0 -> x29, waiting for transfers between devices: none -> 298 us  [the longest x24 211 us: swap_dp(): return lax.ppermute(rows, 'dp', [(i, i ^ 1 << bit) for i in range(size)])]
    psum x3 -> x0, waiting for transfers between devices: 165 us -> none  [the longest x1 58.3 us: on_device(): block_out = residual + lax.psum(ffn_part, 'tensor')]
    reduce_scatter x2 -> x0, waiting for transfers between devices: 128 us -> none  [the longest x1 64 us: on_device(): lax.psum_scatter(q_weight_grad, 'dp', scatter_dimension=0, tiled=True)]
    unnamed x1 -> x0, blocking collectives: 61.3 us -> none
    ppermute x0 -> x29, starting transfers between devices: none -> 37.2 us  [the longest x24 30.2 us: swap_dp(): return lax.ppermute(rows, 'dp', [(i, i ^ 1 << bit) for i in range(size)])]
    dot_general x19 -> x20, matrix products: 51.2 us -> 68.4 us  [the longest x5 23.4 us: scatter_sum(): jnp.einsum('td,tf->df', kept_rows, features, preferred_element_type=jnp.f...]
    slice x0 -> x23, local copies, waits for them, and re-layouts: none -> 10.1 us  [the longest x15 7.4 us: scatter_sum(): total = total[:half] + swap_dp(total[half:], bit)]
  transfers between devices with their start and end apart: 10 -> 29, of which waited for: 9 -> 16; matrix products, arithmetic and copies ran while one was open for 6% -> 24% of each run, Pallas kernels for 0% -> 0%
where the time goes in v1:
time: 507 us; the launch traced here: 502 us
  waiting for transfers between devices  298 us (59%)
  matrix products  98.4 us (19%)
  other arithmetic  45.9 us (9%)
  starting transfers between devices  37.2 us (7%)
  local copies, waits for them, and re-layouts  20.9 us (4%)
    ppermute x24, waiting for transfers between devices, swap_dp(): return lax.ppermute(rows, 'dp', [(i, i ^ 1 << bit) for i in range(size)])  211 us
    ppermute x5, waiting for transfers between devices, swap_tensor(): return lax.ppermute(rows, 'tensor', [(i, i ^ 1) for i in range(size)])  87.5 us
    ppermute x24, starting transfers between devices, swap_dp(): return lax.ppermute(rows, 'dp', [(i, i ^ 1 << bit) for i in range(size)])  30.2 us
    dot_general x5, matrix products, scatter_sum(): jnp.einsum('td,tf->df', kept_rows, features, preferred_element_type=jnp.f...  23.4 us
    dot_general x5, matrix products, scatter_sum(): jnp.einsum('td,tf->df', sent_rows, features, preferred_element_type=jnp.f...  22.2 us
  transfers between devices with their start and end apart: 29, of which 16 were waited for; matrix products, arithmetic and copies ran while one was open for 24% of the time, Pallas kernels for 0%

profile of v1, /device:TPU:0, one launch (start us, length us, event | category | flops | bytes accessed | tf_op | source)
XLA Modules:
  0.0 502.4 jit_solution(5952277739838934291)
XLA Ops:
  28.4 7.1 %fusion.131 = f32[512,2432]{1,0:T(8,128)} fusion(bf16[2432,896]{1,0:T(8,128)(2,1)} %param.29, bf16[512,896]{1,0:T(8,128)(2,1)S(1)} %copy-done.10, f32[512]{0:T(512)S(1)} %fusion.125), kind=kOutput, calls=%fused_computation.183 | convolution fusion | flops 2232745984 | bytes 10258432 | tf_op jit(solution)/shard_map/td,fd->tf/dot_general | solution.py:165
  35.5 28.3 %collective-permute-done = f32[512,896]{1,0:T(8,128)} collective-permute-done((f32[512,896]{1,0:T(8,128)}, f32[512,896]{1,0:T(8,128)}, u32[]{:S(2)}, u32[]{:S(2)}) %collective-permute-start) | collective-permute-done | bytes 1835040 | tf_op jit(solution)/shard_map/ppermute | solution.py:56
  70.0 6.4 %multiply_convert_fusion = (bf16[512,2432]{1,0:T(8,128)(2,1)S(1)}, bf16[512,2432]{1,0:T(8,128)(2,1)S(1)}, bf16[512,2432]{1,0:T(8,128)(2,1)S(1)}) fusion(f32[512,2432]{1,0:T(8,128)} %fusion.131, f32[512,2432]{1,0:T(8,128)S(1)} %fusion.143, bf16[512,896]{1,0:T(8,128)(2,1)S(1)} %multiply_convert_fusion.3, bf16[896,2432]{1,0:T(8,128)(2,1)S(1)} %bitcast.156), kind=kOutput, calls=%fused_computation.10 | convolution fusion | flops 2250047488 | bytes 22708224 | tf_op jit(solution)/shard_map/dot_general | solution.py:157
  79.4 4.2 convolution_add_fusion.3
  85.3 4.1 fusion.144
  92.1 6.4 %fusion.87 = f32[448,2432]{1,0:T(8,128)} fusion(bf16[512,2432]{1,0:T(8,128)(2,1)} %copy-done.19, pred[896,896]{1,0:T(32,128)(4,1)} %iota_compare_fusion, bf16[512,896]{1,0:T(8,128)(2,1)} %param.16, f32[512]{0:T(512)} %copy-done.51), kind=kOutput, calls=%fused_computation.100 | convolution fusion | flops 1528332288 | bytes 8226816 | tf_op jit(solution)/shard_map/td,tf->df/dot_general | solution.py:84
  104.9 21.9 %collective-permute-done.2 = f32[512,896]{1,0:T(8,128)} collective-permute-done((f32[512,896]{1,0:T(8,128)}, f32[512,896]{1,0:T(8,128)}, u32[]{:S(2)}, u32[]{:S(2)}) %collective-permute-start.2) | collective-permute-done | bytes 1835040 | tf_op jit(solution)/shard_map/ppermute | solution.py:56
  130.1 34.2 %collective-permute-done.1 = f32[512,896]{1,0:T(8,128)} collective-permute-done((f32[512,896]{1,0:T(8,128)}, f32[512,896]{1,0:T(8,128)}, u32[]{:S(2)}, u32[]{:S(2)}) %collective-permute-start.1) | collective-permute-done | bytes 1835040 | tf_op jit(solution)/shard_map/ppermute | solution.py:56
  164.4 4.5 fusion.13
  207.4 5.3 %fusion.147 = f32[448,2432]{1,0:T(8,128)} fusion(bf16[512,448]{0,1:T(8,128)(2,1)} %copy-done.20, bf16[512,2432]{1,0:T(8,128)(2,1)} %copy-done.6), kind=kOutput, calls=%fused_computation.191 | convolution fusion | flops 1115684864 | bytes 7307264 | tf_op jit(solution)/shard_map/td,tf->df/dot_general | solution.py:84
  213.4 5.3 %collective-permute-done.14 = f32[224,448]{1,0:T(8,128)} collective-permute-done((f32[224,448]{1,0:T(8,128)}, f32[224,448]{1,0:T(8,128)}, u32[]{:S(2)}, u32[]{:S(2)}) %collective-permute-start.14) | collective-permute-done | bytes 401440 | tf_op jit(solution)/shard_map/ppermute | solution.py:61
  223.4 4.0 convolution_add_fusion.5
  228.5 6.3 %collective-permute-done.15 = f32[112,448]{1,0:T(8,128)} collective-permute-done((f32[112,448]{1,0:T(8,128)S(1)}, f32[112,448]{1,0:T(8,128)}, u32[]{:S(2)}, u32[]{:S(2)}) %collective-permute-start.15) | collective-permute-done | bytes 200736 | tf_op jit(solution)/shard_map/ppermute | solution.py:61
  241.1 8.2 %collective-permute-done.5 = f32[224,576]{1,0:T(8,128)S(1)} collective-permute-done((f32[224,576]{1,0:T(8,128)S(1)}, f32[224,576]{1,0:T(8,128)S(1)}, u32[]{:S(2)}, u32[]{:S(2)}) %collective-permute-start.5) | collective-permute-done | bytes 516128 | tf_op jit(solution)/shard_map/ppermute | solution.py:61
  258.4 8.7 %collective-permute-done.6 = f32[112,576]{1,0:T(8,128)S(1)} collective-permute-done((f32[112,576]{1,0:T(8,128)S(1)}, f32[112,576]{1,0:T(8,128)S(1)}, u32[]{:S(2)}, u32[]{:S(2)}) %collective-permute-start.6) | collective-permute-done | bytes 258080 | tf_op jit(solution)/shard_map/ppermute | solution.py:61
  275.1 7.5 %convolution_add_fusion = f32[448,2432]{1,0:T(8,128)} fusion(f32[448,2432]{1,0:T(8,128)} %collective-permute-done.25, bf16[512,2432]{1,0:T(8,128)(2,1)} %copy-done.19, pred[896,896]{1,0:T(32,128)(4,1)} %iota_compare_fusion, bf16[512,896]{1,0:T(8,128)(2,1)} %param.16, f32[512]{0:T(512)} %copy-done.51), kind=kOutput, calls=%fused_computation.15 | convolution fusion | flops 1529421824 | bytes 12584960 | tf_op jit(solution)/shard_map/td,tf->df/dot_general | solution.py:86
  291.6 4.4 convolution_add_fusion.1
  298.9 3.9 convolution_add_fusion.2
  305.8 30.7 %collective-permute-done.26 = f32[224,2432]{1,0:T(8,128)} collective-permute-done((f32[224,2432]{1,0:T(8,128)}, f32[224,2432]{1,0:T(8,128)}, u32[]{:S(2)}, u32[]{:S(2)}) %collective-permute-start.26) | collective-permute-done | bytes 2179104 | tf_op jit(solution)/shard_map/ppermute | solution.py:61
  340.6 42.5 %collective-permute-done.22 = f32[224,2432]{1,0:T(8,128)S(1)} collective-permute-done((f32[224,2432]{1,0:T(8,128)S(1)}, f32[224,2432]{1,0:T(8,128)S(1)}, u32[]{:S(2)}, u32[]{:S(2)}) %collective-permute-start.22) | collective-permute-done | bytes 2179104 | tf_op jit(solution)/shard_map/ppermute | solution.py:61
  385.4 41.9 %collective-permute-done.18 = f32[224,2432]{1,0:T(8,128)S(1)} collective-permute-done((f32[224,2432]{1,0:T(8,128)S(1)}, f32[224,2432]{1,0:T(8,128)S(1)}, u32[]{:S(2)}, u32[]{:S(2)}) %collective-permute-start.18) | collective-permute-done | bytes 2179104 | tf_op jit(solution)/shard_map/ppermute | solution.py:61
  433.3 39.4 %collective-permute-done.19 = f32[112,2432]{1,0:T(8,128)S(1)} collective-permute-done((f32[112,2432]{1,0:T(8,128)S(1)}, f32[112,2432]{1,0:T(8,128)S(1)}, u32[]{:S(2)}, u32[]{:S(2)}) %collective-permute-start.19) | collective-permute-done | bytes 1089568 | tf_op jit(solution)/shard_map/ppermute | solution.py:61
  476.2 16.0 %collective-permute-done.24 = f32[56,2432]{1,0:T(8,128)S(1)} collective-permute-done((f32[56,2432]{1,0:T(8,128)S(1)}, f32[56,2432]{1,0:T(8,128)S(1)}, u32[]{:S(2)}, u32[]{:S(2)}) %collective-permute-start.24) | collective-permute-done | bytes 544800 | tf_op jit(solution)/shard_map/ppermute | solution.py:61
  493.0 8.2 %collective-permute-done.20 = f32[56,2432]{1,0:T(8,128)S(1)} collective-permute-done((f32[56,2432]{1,0:T(8,128)S(1)}, f32[56,2432]{1,0:T(8,128)S(1)}, u32[]{:S(2)}, u32[]{:S(2)}) %collective-permute-start.20) | collective-permute-done | bytes 544800 | tf_op jit(solution)/shard_map/ppermute | solution.py:61
  (296 shorter events, 151.0 us)
Async XLA Ops:
  20.6 43.3 %collective-permute-start = (f32[512,896]{1,0:T(8,128)}, f32[512,896]{1,0:T(8,128)}, u32[]{:S(2)}, u32[]{:S(2)}) collective-permute-start(f32[512,896]{1,0:T(8,128)} %fusion.142), channel_id=1, source_target_pairs={{0,1},{1,0},{2,3},{3,2},{4,5},{5,4},{6,7},{7,6},{8,9},{9,8},{10,11... | collective-permute-start | bytes 5505032 | tf_op jit(solution)/shard_map/ppermute | solution.py:56
  83.6 43.2 %collective-permute-start.2 = (f32[512,896]{1,0:T(8,128)}, f32[512,896]{1,0:T(8,128)}, u32[]{:S(2)}, u32[]{:S(2)}) collective-permute-start(f32[512,896]{1,0:T(8,128)} %convolution_add_fusion.3), channel_id=1, source_target_pairs={{0,1},{1,0},{2,3},{3,2},{4,5},{5,4},{6,7},{7,6},{8,9},{9,8},{10,11... | collective-permute-start | bytes 5505032 | tf_op jit(solution)/shard_map/ppermute | solution.py:56
  89.4 74.9 %collective-permute-start.1 = (f32[512,896]{1,0:T(8,128)}, f32[512,896]{1,0:T(8,128)}, u32[]{:S(2)}, u32[]{:S(2)}) collective-permute-start(f32[512,896]{1,0:T(8,128)} %fusion.144), channel_id=1, source_target_pairs={{0,1},{1,0},{2,3},{3,2},{4,5},{5,4},{6,7},{7,6},{8,9},{9,8},{10,11... | collective-permute-start | bytes 5505032 | tf_op jit(solution)/shard_map/ppermute | solution.py:56
  98.5 176.7 %collective-permute-start.25 = (f32[448,2432]{1,0:T(8,128)}, f32[448,2432]{1,0:T(8,128)}, u32[]{:S(2)}, u32[]{:S(2)}) collective-permute-start(f32[448,2432]{1,0:T(8,128)} %fusion.87), channel_id=1, source_target_pairs={{0,2},{2,0},{4,6},{6,4},{8,10},{10,8},{12,14},{14,12},{16,18},{18,... | collective-permute-start | bytes 13074440 | tf_op jit(solution)/shard_map/ppermute | solution.py:61
  186.9 13.4 %collective-permute-start.13 = (f32[448,448]{1,0:T(8,128)}, f32[448,448]{1,0:T(8,128)}, u32[]{:S(2)}, u32[]{:S(2)}) collective-permute-start(f32[448,448]{1,0:T(8,128)} %fusion.72), channel_id=1, source_target_pairs={{0,2},{2,0},{4,6},{6,4},{8,10},{10,8},{12,14},{14,12},{16,18},{18,... | collective-permute-start | bytes 2408456 | tf_op jit(solution)/shard_map/ppermute | solution.py:61
  192.5 43.9 %collective-permute-start.3 = (f32[512,896]{1,0:T(8,128)}, f32[512,896]{1,0:T(8,128)}, u32[]{:S(2)}, u32[]{:S(2)}) collective-permute-start(f32[512,896]{1,0:T(8,128)} %fusion.146), channel_id=1, source_target_pairs={{0,1},{1,0},{2,3},{3,2},{4,5},{5,4},{6,7},{7,6},{8,9},{9,8},{10,11... | collective-permute-start | bytes 5505032 | tf_op jit(solution)/shard_map/ppermute | solution.py:56
  197.7 23.0 %collective-permute-start.4 = (f32[448,576]{1,0:T(8,128)}, f32[448,576]{1,0:T(8,128)}, u32[]{:S(2)}, u32[]{:S(2)}) collective-permute-start(f32[448,576]{1,0:T(8,128)} %fusion.75), channel_id=1, source_target_pairs={{0,2},{2,0},{4,6},{6,4},{8,10},{10,8},{12,14},{14,12},{16,18},{18,... | collective-permute-start | bytes 3096584 | tf_op jit(solution)/shard_map/ppermute | solution.py:61
  199.9 91.6 %collective-permute-start.21 = (f32[448,2432]{1,0:T(8,128)}, f32[448,2432]{1,0:T(8,128)}, u32[]{:S(2)}, u32[]{:S(2)}) collective-permute-start(f32[448,2432]{1,0:T(8,128)} %fusion.148), channel_id=1, source_target_pairs={{0,2},{2,0},{4,6},{6,4},{8,10},{10,8},{12,14},{14,12},{16,18},{18,... | collective-permute-start | bytes 13074440 | tf_op jit(solution)/shard_map/ppermute | solution.py:61
  218.7 80.2 %collective-permute-start.17 = (f32[448,2432]{1,0:T(8,128)}, f32[448,2432]{1,0:T(8,128)}, u32[]{:S(2)}, u32[]{:S(2)}) collective-permute-start(f32[448,2432]{1,0:T(8,128)} %fusion.147), channel_id=1, source_target_pairs={{0,2},{2,0},{4,6},{6,4},{8,10},{10,8},{12,14},{14,12},{16,18},{18,... | collective-permute-start | bytes 13074440 | tf_op jit(solution)/shard_map/ppermute | solution.py:61
  220.7 14.0 %collective-permute-start.15 = (f32[112,448]{1,0:T(8,128)S(1)}, f32[112,448]{1,0:T(8,128)}, u32[]{:S(2)}, u32[]{:S(2)}) collective-permute-start(f32[112,448]{1,0:T(8,128)S(1)} %slice.240), channel_id=1, source_target_pairs={{0,16},{2,18},{4,20},{6,22},{8,24},{10,26},{12,28},{14,30},{16,0},... | collective-permute-start | bytes 602120 | tf_op jit(solution)/shard_map/ppermute | solution.py:61
  234.7 14.5 %collective-permute-start.5 = (f32[224,576]{1,0:T(8,128)S(1)}, f32[224,576]{1,0:T(8,128)S(1)}, u32[]{:S(2)}, u32[]{:S(2)}) collective-permute-start(f32[224,576]{1,0:T(8,128)S(1)} %slice.227), channel_id=1, source_target_pairs={{0,8},{2,10},{4,12},{6,14},{8,0},{10,2},{12,4},{14,6},{16,24},{18,... | collective-permute-start | bytes 1548296 | tf_op jit(solution)/shard_map/ppermute | solution.py:61
  236.4 19.2 %collective-permute-start.16 = (f32[56,448]{1,0:T(8,128)S(1)}, f32[56,448]{1,0:T(8,128)S(1)}, u32[]{:S(2)}, u32[]{:S(2)}) collective-permute-start(f32[56,448]{1,0:T(8,128)S(1)} %slice.242), channel_id=1, source_target_pairs={{0,4},{2,6},{4,0},{6,2},{8,12},{10,14},{12,8},{14,10},{16,20},{18,... | collective-permute-start | bytes 301064 | tf_op jit(solution)/shard_map/ppermute | solution.py:61
  252.9 14.2 %collective-permute-start.6 = (f32[112,576]{1,0:T(8,128)S(1)}, f32[112,576]{1,0:T(8,128)S(1)}, u32[]{:S(2)}, u32[]{:S(2)}) collective-permute-start(f32[112,576]{1,0:T(8,128)S(1)} %slice.229), channel_id=1, source_target_pairs={{0,16},{2,18},{4,20},{6,22},{8,24},{10,26},{12,28},{14,30},{16,0},... | collective-permute-start | bytes 774152 | tf_op jit(solution)/shard_map/ppermute | solution.py:61
  267.8 35.7 %collective-permute-start.7 = (f32[56,576]{1,0:T(8,128)}, f32[56,576]{1,0:T(8,128)}, u32[]{:S(2)}, u32[]{:S(2)}) collective-permute-start(f32[56,576]{1,0:T(8,128)} %slice.231), channel_id=1, source_target_pairs={{0,4},{2,6},{4,0},{6,2},{8,12},{10,14},{12,8},{14,10},{16,20},{18,... | collective-permute-start | bytes 387080 | tf_op jit(solution)/shard_map/ppermute | solution.py:61
  273.1 17.1 %collective-permute-start.12 = (f32[2368]{0:T(1024)S(1)}, f32[2368]{0:T(1024)S(1)}, u32[]{:S(2)}, u32[]{:S(2)}) collective-permute-start(f32[2368]{0:T(1024)S(1)} %add.272), channel_id=1, source_target_pairs={{0,16},{2,18},{4,20},{6,22},{8,24},{10,26},{12,28},{14,30},{16,0},... | collective-permute-start | bytes 28424 | tf_op jit(solution)/shard_map/ppermute | solution.py:61
  285.9 50.6 %collective-permute-start.26 = (f32[224,2432]{1,0:T(8,128)}, f32[224,2432]{1,0:T(8,128)}, u32[]{:S(2)}, u32[]{:S(2)}) collective-permute-start(f32[224,2432]{1,0:T(8,128)} %slice.258), channel_id=1, source_target_pairs={{0,4},{2,6},{4,0},{6,2},{8,12},{10,14},{12,8},{14,10},{16,20},{18,... | collective-permute-start | bytes 6537224 | tf_op jit(solution)/shard_map/ppermute | solution.py:61
  296.1 86.9 %collective-permute-start.22 = (f32[224,2432]{1,0:T(8,128)S(1)}, f32[224,2432]{1,0:T(8,128)S(1)}, u32[]{:S(2)}, u32[]{:S(2)}) collective-permute-start(f32[224,2432]{1,0:T(8,128)S(1)} %slice.252), channel_id=1, source_target_pairs={{0,4},{2,6},{4,0},{6,2},{8,12},{10,14},{12,8},{14,10},{16,20},{18,... | collective-permute-start | bytes 6537224 | tf_op jit(solution)/shard_map/ppermute | solution.py:61
  303.0 124.4 %collective-permute-start.18 = (f32[224,2432]{1,0:T(8,128)S(1)}, f32[224,2432]{1,0:T(8,128)S(1)}, u32[]{:S(2)}, u32[]{:S(2)}) collective-permute-start(f32[224,2432]{1,0:T(8,128)S(1)} %slice.246), channel_id=1, source_target_pairs={{0,4},{2,6},{4,0},{6,2},{8,12},{10,14},{12,8},{14,10},{16,20},{18,... | collective-permute-start | bytes 6537224 | tf_op jit(solution)/shard_map/ppermute | solution.py:61
  338.5 91.4 %collective-permute-start.27 = (f32[112,2432]{1,0:T(8,128)S(1)}, f32[112,2432]{1,0:T(8,128)S(1)}, u32[]{:S(2)}, u32[]{:S(2)}) collective-permute-start(f32[112,2432]{1,0:T(8,128)S(1)} %slice.260), channel_id=1, source_target_pairs={{0,8},{2,10},{4,12},{6,14},{8,0},{10,2},{12,4},{14,6},{16,24},{18,... | collective-permute-start | bytes 3268616 | tf_op jit(solution)/shard_map/ppermute | solution.py:61
  383.3 47.1 %collective-permute-start.23 = (f32[112,2432]{1,0:T(8,128)S(1)}, f32[112,2432]{1,0:T(8,128)S(1)}, u32[]{:S(2)}, u32[]{:S(2)}) collective-permute-start(f32[112,2432]{1,0:T(8,128)S(1)} %slice.254), channel_id=1, source_target_pairs={{0,8},{2,10},{4,12},{6,14},{8,0},{10,2},{12,4},{14,6},{16,24},{18,... | collective-permute-start | bytes 3268616 | tf_op jit(solution)/shard_map/ppermute | solution.py:61
  427.7 45.0 %collective-permute-start.19 = (f32[112,2432]{1,0:T(8,128)S(1)}, f32[112,2432]{1,0:T(8,128)S(1)}, u32[]{:S(2)}, u32[]{:S(2)}) collective-permute-start(f32[112,2432]{1,0:T(8,128)S(1)} %slice.248), channel_id=1, source_target_pairs={{0,8},{2,10},{4,12},{6,14},{8,0},{10,2},{12,4},{14,6},{16,24},{18,... | collective-permute-start | bytes 3268616 | tf_op jit(solution)/shard_map/ppermute | solution.py:61
  430.1 45.3 %collective-permute-start.28 = (f32[56,2432]{1,0:T(8,128)S(1)}, f32[56,2432]{1,0:T(8,128)S(1)}, u32[]{:S(2)}, u32[]{:S(2)}) collective-permute-start(f32[56,2432]{1,0:T(8,128)S(1)} %slice.262), channel_id=1, source_target_pairs={{0,16},{2,18},{4,20},{6,22},{8,24},{10,26},{12,28},{14,30},{16,0},... | collective-permute-start | bytes 1634312 | tf_op jit(solution)/shard_map/ppermute | solution.py:61
  430.6 61.6 %collective-permute-start.24 = (f32[56,2432]{1,0:T(8,128)S(1)}, f32[56,2432]{1,0:T(8,128)S(1)}, u32[]{:S(2)}, u32[]{:S(2)}) collective-permute-start(f32[56,2432]{1,0:T(8,128)S(1)} %slice.256), channel_id=1, source_target_pairs={{0,16},{2,18},{4,20},{6,22},{8,24},{10,26},{12,28},{14,30},{16,0},... | collective-permute-start | bytes 1634312 | tf_op jit(solution)/shard_map/ppermute | solution.py:61
  472.9 28.4 %collective-permute-start.20 = (f32[56,2432]{1,0:T(8,128)S(1)}, f32[56,2432]{1,0:T(8,128)S(1)}, u32[]{:S(2)}, u32[]{:S(2)}) collective-permute-start(f32[56,2432]{1,0:T(8,128)S(1)} %slice.250), channel_id=1, source_target_pairs={{0,16},{2,18},{4,20},{6,22},{8,24},{10,26},{12,28},{14,30},{16,0},... | collective-permute-start | bytes 1634312 | tf_op jit(solution)/shard_map/ppermute | solution.py:61
  (77 other events, 861.4 us)

commit v2 on v1

--- a/solution.py
+++ b/solution.py
@@ -1,8 +1,11 @@
+import functools
 import math
 
 import jax
 import jax.numpy as jnp
 from jax import lax
+from jax.experimental import pallas as pl
+from jax.experimental.pallas import tpu as pltpu
 from jax.sharding import PartitionSpec as P
 
 HD = 64
@@ -61,33 +64,113 @@
     return lax.ppermute(rows, "dp", [(i, i ^ (1 << bit)) for i in range(size)])
 
 
-def dest_columns(width, order):
+def after(value, *others):
+    return lax.optimization_barrier((value, *others))[0]
+
+
+def dest_columns(width, order, fixed=()):
     steps = len(order)
-    blocks = 1 << steps
-    block = width // blocks
+    block = width >> (steps + len(fixed))
+    count = block << steps
     own = lax.axis_index("dp")
-    places = jnp.arange(width, dtype=jnp.int32)
+    places = jnp.arange(count, dtype=jnp.int32)
     spot = places // block
     flip = jnp.zeros_like(spot)
     for j, bit in enumerate(order):
         flip = flip + (((spot >> (steps - 1 - j)) & 1) << bit)
     source = (own ^ flip) * block + places % block
     chosen = (jnp.arange(width, dtype=jnp.int32)[:, None] == source[None, :]).astype(jnp.bfloat16)
-    return chosen[:, : width // 2], chosen[:, width // 2 :]
+    return chosen[:, : count // 2], chosen[:, count // 2 :]
 
 
 def pick(rows, chosen):
     return jnp.dot(rows, chosen, preferred_element_type=jnp.float32).astype(jnp.bfloat16)
 
 
+def outer(rows, features):
+    return jnp.einsum("td,tf->df", rows, features, preferred_element_type=jnp.float32)
+
+
+def fold(kept_rows, features, sent):
+    kept_rows = after(kept_rows, sent)
+    half = sent.shape[0] // 2
+    keep = outer(kept_rows[:, :half], features) + sent[:half]
+    send = outer(kept_rows[:, half:], features) + sent[half:]
+    return keep, send
+
+
+def finish(keep, send, order):
+    for bit in order[:-1]:
+        sent = swap_dp(send, bit)
+        half = sent.shape[0] // 2
+        send = keep[half:] + sent[half:]
+        keep = keep[:half] + sent[:half]
+    return keep + swap_dp(send, order[-1])
+
+
 def scatter_sum(kept_rows, sent_rows, features, order):
-    sent = jnp.einsum("td,tf->df", sent_rows, features, preferred_element_type=jnp.float32)
-    sent = swap_dp(sent, order[0])
-    total = jnp.einsum("td,tf->df", kept_rows, features, preferred_element_type=jnp.float32) + sent
-    for bit in order[1:]:
-        half = total.shape[0] // 2
-        total = total[:half] + swap_dp(total[half:], bit)
-    return total
+    keep, send = fold(kept_rows, features, swap_dp(outer(sent_rows, features), order[0]))
+    return finish(keep, send, order[1:])
+
+
+IN_VMEM = pl.BlockSpec(memory_space=pltpu.VMEM)
+
+
+def contract(left, right, left_dim, right_dim):
+    return lax.dot_general(
+        left, right, (((left_dim,), (right_dim,)), ((), ())), preferred_element_type=jnp.float32
+    )
+
+
+def over(total, size, step):
+    count, rest = divmod(total, size)
+
+    def turn(i, carry):
+        step(pl.multiple_of(i * size, size), size)
+        return carry
+
+    lax.fori_loop(0, count, turn, 0)
+    if rest:
+        step(count * size, rest)
+
+
+def ffn_kernel(two_ref, branch_ref, gate_ref, up_ref, down_ref, hidden_ref, gate_rows_ref, up_rows_ref, *own_refs):
+    def forth(start, size):
+        c = pl.ds(start, size)
+        gate = contract(two_ref[...], gate_ref[:, c], 1, 0)
+        up = contract(two_ref[...], up_ref[:, c], 1, 0)
+        hidden_grad = contract(branch_ref[...], down_ref[c, :], 1, 1)
+        sigmoid_gate = 0.5 * jnp.tanh(0.5 * gate) + 0.5
+        silu_gate = gate * sigmoid_gate
+        hidden_ref[:, c] = (silu_gate * up).astype(jnp.bfloat16)
+        gate_rows_ref[:, c] = (hidden_grad * up * (sigmoid_gate + silu_gate * (1.0 - sigmoid_gate))).astype(jnp.bfloat16)
+        up_rows_ref[:, c] = (hidden_grad * silu_gate).astype(jnp.bfloat16)
+
+    def back(start, size):
+        part_ref, ffn_ref = own_refs
+        c = pl.ds(start, size)
+        part_ref[:, c] = contract(gate_rows_ref[...], gate_ref[c, :], 1, 1) + contract(
+            up_rows_ref[...], up_ref[c, :], 1, 1
+        )
+        ffn_ref[:, c] = contract(hidden_ref[...], down_ref[:, c], 1, 0)
+
+    over(gate_ref.shape[1], 768, forth)
+    if own_refs:
+        over(gate_ref.shape[0], 256, back)
+
+
+def ffn_rows(rows, branch, gate_weight, up_weight, down_weight, own):
+    count, width = rows.shape
+    wide = jax.ShapeDtypeStruct((count, gate_weight.shape[1]), jnp.bfloat16)
+    total = jax.ShapeDtypeStruct((count, width), jnp.float32)
+    return pl.pallas_call(
+        ffn_kernel,
+        in_specs=[IN_VMEM] * 5,
+        out_specs=[IN_VMEM] * (5 if own else 3),
+        out_shape=[wide] * 3 + [total] * (2 if own else 0),
+        compiler_params=pltpu.CompilerParams(vmem_limit_bytes=40 * 2**20),
+        name="ffn_own" if own else "ffn_pair",
+    )(rows, branch, gate_weight, up_weight, down_weight)
 
 
 def on_device(
@@ -113,14 +196,28 @@
     group_size = local_heads // local_kv
     dp_size = lax.axis_size("dp")
     dp_bits = dp_size.bit_length() - 1
-    ffn_order = tuple(range(dp_bits))
-    attn_order = (0,) + tuple(range(2, dp_bits)) + (1,)
+    pair_bit = 2
+    ffn_order = (0, 1) + tuple(range(3, dp_bits))
+    attn_order = (0, pair_bit, 1) + tuple(range(3, dp_bits))
     own = lax.axis_index("dp")
     score_scale = HD ** (-0.5)
     segment, positions, alive = layout(doc_lengths[0], row_total)
     cosine, sine_table = rotary(positions, HD)
     alive_rows = alive.astype(jnp.float32)[:, None]
     places = jnp.arange(row_total, dtype=jnp.int32)
+    unit = alive_rows[0, 0]
+    o_half = o_weight.shape[0] // 2
+    o_first = own & 1
+    upstream = out_grad.astype(jnp.float32)
+    branch_wide = upstream * alive_rows
+    o_mine = lax.dynamic_slice_in_dim(o_weight, o_first * o_half, o_half).astype(jnp.float32)
+    o_same = swap_tensor(o_mine)
+    pair_branch = (swap_dp(branch_wide, pair_bit) * unit).astype(jnp.bfloat16)
+    o_cross = swap_dp(o_same, 0) * unit
+    o_same = o_same * unit
+    o_low = jnp.where(o_first == 0, o_same, o_cross).astype(jnp.bfloat16)
+    o_high = jnp.where(o_first == 0, o_cross, o_same).astype(jnp.bfloat16)
+    branch_grad = branch_wide.astype(jnp.bfloat16)
     inputs = tokens.astype(jnp.float32)
     gain_one = attn_gain.astype(jnp.float32)
     gain_two = ffn_gain.astype(jnp.float32)
@@ -150,32 +247,46 @@
         .reshape(row_total, q_width)
         .astype(jnp.bfloat16)
     )
-    attn_part = jnp.dot(mixed_heads, o_weight, preferred_element_type=jnp.float32)
-    residual = inputs + (attn_part + swap_tensor(attn_part))
+    mixed_other = (swap_tensor(mixed_heads.astype(jnp.float32)) * unit).astype(jnp.bfloat16)
+    residual = inputs + (
+        jnp.dot(mixed_heads, o_weight, preferred_element_type=jnp.float32)
+        + jnp.dot(
+            mixed_other, jnp.concatenate([o_low, o_high]), preferred_element_type=jnp.float32
+        )
+    )
     factor_two = lax.rsqrt(jnp.mean(residual * residual, axis=-1, keepdims=True) + norm_eps)
     normed_two = (residual * factor_two * gain_two).astype(jnp.bfloat16)
-    gate_act = jnp.dot(normed_two, gate_weight, preferred_element_type=jnp.float32)
-    up_act = jnp.dot(normed_two, up_weight, preferred_element_type=jnp.float32)
-    hidden_act = (jax.nn.silu(gate_act) * up_act).astype(jnp.bfloat16)
-    upstream = out_grad.astype(jnp.float32)
-    branch_grad = (upstream * alive_rows).astype(jnp.bfloat16)
-    ffn_keep, ffn_send = dest_columns(width, ffn_order)
+    pair_two = (swap_dp(normed_two.astype(jnp.float32), pair_bit) * unit).astype(jnp.bfloat16)
+
+    hidden_act, gate_grad_rows, up_grad_rows, normed_two_part, ffn_part = ffn_rows(
+        normed_two, branch_grad, gate_weight, up_weight, down_weight, True
+    )
+    two_from_x = swap_tensor(normed_two_part)
+    ffn_gain_part = jnp.sum(normed_two_part * (residual * factor_two), axis=0)
+
+    pair_hidden, pair_gate_rows, pair_up_rows = ffn_rows(
+        pair_two, pair_branch, gate_weight, up_weight, down_weight, False
+    )
+    ffn_keep, ffn_send = dest_columns(width, ffn_order, (pair_bit,))
     attn_keep, attn_send = dest_columns(width, attn_order)
-    down_grad = scatter_sum(pick(branch_grad, ffn_keep), pick(branch_grad, ffn_send), hidden_act, ffn_order)
-    hidden_grad = jnp.einsum("td,fd->tf", branch_grad, down_weight, preferred_element_type=jnp.float32)
-    sigmoid_gate = jax.nn.sigmoid(gate_act)
-    gate_grad_rows = (
-        hidden_grad * up_act * (sigmoid_gate * (1.0 + gate_act * (1.0 - sigmoid_gate)))
-    ).astype(jnp.bfloat16)
-    up_grad_rows = (hidden_grad * jax.nn.silu(gate_act)).astype(jnp.bfloat16)
-    normed_two_part = jnp.einsum(
-        "tf,df->td", gate_grad_rows, gate_weight, preferred_element_type=jnp.float32
-    ) + jnp.einsum("tf,df->td", up_grad_rows, up_weight, preferred_element_type=jnp.float32)
-    two_keep, two_send = pick(normed_two, ffn_keep), pick(normed_two, ffn_send)
-    gate_grad = scatter_sum(two_keep, two_send, gate_grad_rows, ffn_order)
-    up_grad = scatter_sum(two_keep, two_send, up_grad_rows, ffn_order)
-    normed_two_grad = normed_two_part + swap_tensor(normed_two_part)
-    ffn_gain_part = jnp.sum(normed_two_part * (residual * factor_two), axis=0)
+    both_branch = jnp.concatenate([branch_grad, pair_branch])
+    both_two = jnp.concatenate([normed_two, pair_two])
+    both_hidden = jnp.concatenate([hidden_act, pair_hidden])
+    both_gate = jnp.concatenate([gate_grad_rows, pair_gate_rows])
+    both_up = jnp.concatenate([up_grad_rows, pair_up_rows])
+    branch_keep, branch_send = pick(both_branch, ffn_keep), pick(both_branch, ffn_send)
+    two_keep, two_send = pick(both_two, ffn_keep), pick(both_two, ffn_send)
+    down_sent = swap_dp(outer(branch_send, both_hidden), 0)
+    gate_sent = swap_dp(outer(two_send, both_gate), 0)
+    up_sent = swap_dp(outer(two_send, both_up), 0)
+    down_parts = fold(branch_keep, both_hidden, down_sent)
+    gate_parts = fold(after(two_keep, *down_parts), both_gate, gate_sent)
+    up_parts = fold(after(two_keep, *gate_parts), both_up, up_sent)
+    down_grad = finish(*down_parts, ffn_order[1:])
+    gate_grad = finish(*gate_parts, ffn_order[1:])
+    up_grad = finish(*up_parts, ffn_order[1:])
+    two_from_x = after(two_from_x, *up_parts)
+    normed_two_grad = normed_two_part + two_from_x
     residual_grad = norm_back(residual, factor_two, gain_two, normed_two_grad)
     residual_grad = residual_grad + upstream * alive_rows
     residual_low = residual_grad.astype(jnp.bfloat16)
@@ -219,7 +330,7 @@
     bias_heads = small[2 * width :].reshape(local_heads + 2 * local_kv, HD)
     bias_block = HD // dp_size
     bias_own = lax.dynamic_slice_in_dim(bias_heads, own * bias_block, bias_block, axis=1)
-    ffn_part = jnp.dot(hidden_act, down_weight, preferred_element_type=jnp.float32)
+    ffn_part = after(ffn_part, two_from_x)
     block_out = residual + (ffn_part + swap_tensor(ffn_part))
     layer_out = jnp.where(alive[:, None], block_out, inputs).astype(jnp.bfloat16)
     return (

time: 507 us -> 386 us (0.76)
  waiting for transfers between devices: 298 us -> 169 us
  Pallas kernels: 0 us -> 35.6 us
  matrix products: 98.4 us -> 75.7 us
  other arithmetic: 45.9 us -> 38 us
    ppermute x24, waiting for transfers between devices: 211 us -> 121 us  [swap_dp(): return lax.ppermute(rows, 'dp', [(i, i ^ 1 << bit) for i in range(size)])]
    ppermute x5 -> x6, waiting for transfers between devices: 87.5 us -> 47.4 us  [swap_tensor(): return lax.ppermute(rows, 'tensor', [(i, i ^ 1) for i in range(size)])]
    pallas_call x0 -> x2, Pallas kernels: none -> 35.6 us  [ffn_rows(): pl.pallas_call(ffn_kernel, in_specs=[IN_VMEM] * 5, out_specs=[IN_VMEM] *...]
    dot_general x16, matrix products: 73 us -> 47.2 us  [the longest x15 45.6 us: outer(): jnp.einsum('td,tf->df', rows, features, preferred_element_type=jnp.float32)]
    convert_element_type x1 -> x6, other arithmetic: 0.22 us -> 8.6 us  [the longest x1 2.26 us: on_device(): pair_branch = (swap_dp(branch_wide, pair_bit) * unit).astype(jnp.bfloat16)]
    slice x15 -> x1, local copies, waits for them, and re-layouts: 7.4 us -> 0.51 us  [on_device(): unit = alive_rows[0, 0]]
    concatenate x0 -> x3, local copies, waits for them, and re-layouts: none -> 5.46 us  [the longest x1 3.43 us: on_device(): both_gate = jnp.concatenate([gate_grad_rows, pair_gate_rows])]
  transfers between devices with their start and end apart: 29 -> 30, of which waited for: 16 -> 14; matrix products, arithmetic and copies ran while one was open for 24% -> 25% of each run, Pallas kernels for 0% -> 6%
where the time goes in v2:
time: 386 us; the launch traced here: 381 us
  waiting for transfers between devices  169 us (44%)
  matrix products  75.7 us (20%)
  other arithmetic  38 us (10%)
  starting transfers between devices  37.3 us (10%)
  Pallas kernels  35.6 us (9%)
  local copies, waits for them, and re-layouts  23.6 us (6%)
    ppermute x24, waiting for transfers between devices, swap_dp(): return lax.ppermute(rows, 'dp', [(i, i ^ 1 << bit) for i in range(size)])  121 us
    ppermute x6, waiting for transfers between devices, swap_tensor(): return lax.ppermute(rows, 'tensor', [(i, i ^ 1) for i in range(size)])  47.4 us
    dot_general x15, matrix products, outer(): jnp.einsum('td,tf->df', rows, features, preferred_element_type=jnp.float32)  45.6 us
    pallas_call x2, Pallas kernels, ffn_rows(): pl.pallas_call(ffn_kernel, in_specs=[IN_VMEM] * 5, out_specs=[IN_VMEM] *...  35.6 us
    ppermute x24, starting transfers between devices, swap_dp(): return lax.ppermute(rows, 'dp', [(i, i ^ 1 << bit) for i in range(size)])  29.1 us
    unnamed x147, local copies, waits for them, and re-layouts  13.6 us
    ppermute x6, starting transfers between devices, swap_tensor(): return lax.ppermute(rows, 'tensor', [(i, i ^ 1) for i in range(size)])  8.26 us
  transfers between devices with their start and end apart: 30, of which 14 were waited for; matrix products, arithmetic and copies ran while one was open for 25% of the time, Pallas kernels for 6%

profile of v2, /device:TPU:0, one launch (start us, length us, event | category | flops | bytes accessed | tf_op | source)
XLA Modules:
  0.0 381.2 jit_solution(2310832341216495124)
XLA Ops:
  2.8 3.0 collective-permute-start.1
  16.4 3.6 fusion.45
  32.9 10.7 %collective-permute-done = f32[512,448]{0,1:T(8,128)S(1)} collective-permute-done((f32[512,448]{0,1:T(8,128)}, f32[512,448]{0,1:T(8,128)S(1)}, u32[]{:S(2)}, u32[]{:S(2)}) %collective-permute-start) | collective-permute-done | bytes 917536 | tf_op jit(solution)/shard_map/ppermute | solution.py:59
  51.6 22.6 %ffn_own.1 = (bf16[512,2432]{1,0:T(8,128)(2,1)S(1)}, bf16[512,2432]{1,0:T(8,128)(2,1)S(1)}, bf16[512,2432]{1,0:T(8,128)(2,1)S(1)}, f32[512,896]{1,0:T(8,128)S(1)}, f32[512,896]{1,0:T(8,128)S(1)}) custom-call(bf16[512,896]{1,0:T(8,128)(2,1)S(1)} %get-tuple-element.85.two_ref, bf16[512,896]{1,0:T(8,128)(2,1)S(1)} %copy-done, bf16[896,2432]{1,0:T(8,128)(2,1)} %gate_ref.3, ...), custom_call_target="tpu_custom_call" | custom-call | tf_op jit(solution)/shard_map/ffn_own/pallas_call | solution.py:166
  81.3 27.1 %collective-permute-done.4 = f32[512,896]{1,0:T(8,128)S(1)} collective-permute-done((f32[512,896]{1,0:T(8,128)S(1)}, f32[512,896]{1,0:T(8,128)S(1)}, u32[]{:S(2)}, u32[]{:S(2)}) %collective-permute-start.4) | collective-permute-done | bytes 1835040 | tf_op jit(solution)/shard_map/ppermute | solution.py:64
  109.3 13.0 %ffn_pair.1 = (bf16[512,2432]{1,0:T(8,128)(2,1)S(1)}, bf16[512,2432]{1,0:T(8,128)(2,1)S(1)}, bf16[512,2432]{1,0:T(8,128)(2,1)S(1)}) custom-call(bf16[512,896]{1,0:T(8,128)(2,1)S(1)} %multiply_convert_fusion.1.two_ref, bf16[512,896]{1,0:T(8,128)(2,1)S(1)} %multiply_convert_fusion.branch_ref, bf16[896,2432]{1,0:T(8,128)(2,1)S(1)} %bitcast.130, ...), custom_call_target="tpu_custom_call" | custom-call | tf_op jit(solution)/shard_map/ffn_pair/pallas_call | solution.py:166
  127.0 7.5 %fusion.60 = f32[224,2432]{1,0:T(8,128)} fusion(bf16[1024,2432]{1,0:T(8,128)(2,1)} %constant_dynamic-update-slice_fusion.3, bf16[512,896]{1,0:T(8,128)(2,1)} %copy-done.1, bf16[512,896]{1,0:T(8,128)(2,1)} %get-tuple-element.97.branch_ref, pred[896,448]{1,0:T(32,128)(4,1)} %iota_compare_fusion.1), kind=kOutput, calls=%fused_computation.93 | convolution fusion | flops 1530626048 | bytes 9224192 | tf_op jit(solution)/shard_map/td,tf->df/dot_general | solution.py:91
  134.5 3.4 constant_dynamic-update-slice_fusion.5
  139.0 5.3 %fusion.143 = f32[224,2432]{1,0:T(8,128)} fusion(bf16[1024,224]{0,1:T(8,128)(2,1)S(1)} %convolution_convert_fusion.2, bf16[1024,2432]{1,0:T(8,128)(2,1)} %constant_dynamic-update-slice_fusion.5), kind=kOutput, calls=%fused_computation.227 | convolution fusion | flops 1115684864 | bytes 7618560 | tf_op jit(solution)/shard_map/td,tf->df/dot_general | solution.py:91
  154.5 4.0 %convolution_add_fusion.4 = f32[112,2432]{1,0:T(8,128)S(1)} fusion(bf16[1024,2432]{1,0:T(8,128)(2,1)} %constant_dynamic-update-slice_fusion.3, f32[224,2432]{1,0:T(8,128)} %collective-permute-done.6, bf16[1024,224]{0,1:T(8,128)(2,1)S(1)} %convolution_convert_fusion.3), kind=kOutput, calls=%fused_computation.20 | convolution fusion | flops 558114816 | bytes 7389184 | tf_op jit(solution)/shard_map/td,tf->df/dot_general | solution.py:91
  160.2 3.8 convolution_add_fusion.5
  175.2 16.8 %collective-permute-done.3 = f32[512,896]{1,0:T(8,128)S(1)} collective-permute-done((f32[512,896]{1,0:T(8,128)S(1)}, f32[512,896]{1,0:T(8,128)S(1)}, u32[]{:S(2)}, u32[]{:S(2)}) %collective-permute-start.3) | collective-permute-done | bytes 1835040 | tf_op jit(solution)/shard_map/ppermute | solution.py:59
  197.7 33.8 %collective-permute-done.26 = f32[112,2432]{1,0:T(8,128)S(1)} collective-permute-done((f32[112,2432]{1,0:T(8,128)S(1)}, f32[112,2432]{1,0:T(8,128)S(1)}, u32[]{:S(2)}, u32[]{:S(2)}) %collective-permute-start.26) | collective-permute-done | bytes 1089568 | tf_op jit(solution)/shard_map/ppermute | solution.py:64
  235.6 35.0 %collective-permute-done.27 = f32[56,2432]{1,0:T(8,128)S(1)} collective-permute-done((f32[56,2432]{1,0:T(8,128)S(1)}, f32[56,2432]{1,0:T(8,128)S(1)}, u32[]{:S(2)}, u32[]{:S(2)}) %collective-permute-start.27) | collective-permute-done | bytes 544800 | tf_op jit(solution)/shard_map/ppermute | solution.py:64
  271.5 9.7 %collective-permute-done.25 = f32[56,2432]{1,0:T(8,128)S(1)} collective-permute-done((f32[56,2432]{1,0:T(8,128)S(1)}, f32[56,2432]{1,0:T(8,128)S(1)}, u32[]{:S(2)}, u32[]{:S(2)}) %collective-permute-start.25) | collective-permute-done | bytes 544800 | tf_op jit(solution)/shard_map/ppermute | solution.py:64
  284.5 3.8 %fusion.49 = f32[448,448]{1,0:T(8,128)} fusion(bf16[512,448]{0,1:T(8,128)(2,1)S(1)} %bitcast.140, pred[896,896]{1,0:T(32,128)(4,1)} %copy-done.28, f32[512,896]{1,0:T(8,128)} %get-tuple-element.86), kind=kOutput, calls=%fused_computation.78 | convolution fusion | flops 617250816 | bytes 3555328 | tf_op jit(solution)/shard_map/td,tf->df/dot_general | solution.py:91
  290.2 4.7 %fusion = (f32[7,512]{1,0:T(8,128)S(1)}, f32[512,512,7]{1,0,2:T(8,128)S(1)}) fusion(f32[7,512]{1,0:T(8,128)S(1)} %copy-done.39, f32[7,512]{1,0:T(8,128)S(1)} %get-tuple-element.111, f32[512,512,7]{1,0,2:T(8,128)} %copy-done.10, pred[512,512]{0,1:T(8,128)(4,1)S(1)} %copy-done.25, bf16[512,7,64]{0,2,1:T(8,128)(2,1)S(1)} %bitcast.148, f32[512,576]{0,1:T(8,128)} %copy-done.26), kind=kOutput, calls=%fused_computation.3 | convolution fusion | flops 245887488 | bytes 15509504 | tf_op jit(solution)/shard_map/qkgd,skd->kgqs/dot_general | solution.py:300
  303.5 3.7 fusion.52
  307.7 3.6 fusion.145
  320.4 8.5 %collective-permute-done.21 = f32[224,448]{1,0:T(8,128)S(1)} collective-permute-done((f32[224,448]{1,0:T(8,128)S(1)}, f32[224,448]{1,0:T(8,128)S(1)}, u32[]{:S(2)}, u32[]{:S(2)}) %collective-permute-start.21) | collective-permute-done | bytes 401440 | tf_op jit(solution)/shard_map/ppermute | solution.py:64
  331.9 3.1 collective-permute-done.22
  337.1 16.5 %collective-permute-done.10 = f32[512,896]{1,0:T(8,128)} collective-permute-done((f32[512,896]{1,0:T(8,128)}, f32[512,896]{1,0:T(8,128)}, u32[]{:S(2)}, u32[]{:S(2)}) %collective-permute-start.10) | collective-permute-done | bytes 1835040 | tf_op jit(solution)/shard_map/ppermute | solution.py:59
  365.7 4.0 %collective-permute-start.18 = (f32[2368]{0:T(1024)S(1)}, f32[2368]{0:T(1024)S(1)}, u32[]{:S(2)}, u32[]{:S(2)}) collective-permute-start(f32[2368]{0:T(1024)S(1)} %add.298), channel_id=1, source_target_pairs={{0,8},{2,10},{4,12},{6,14},{8,0},{10,2},{12,4},{14,6},{16,24},{18,... | collective-permute-start | bytes 28424 | tf_op jit(solution)/shard_map/ppermute | solution.py:64
  373.2 3.8 fusion.18
  (294 shorter events, 128.2 us)
Async XLA Ops:
  2.8 21.6 %collective-permute-start.1 = (f32[224,896]{1,0:T(8,128)}, f32[224,896]{1,0:T(8,128)}, u32[]{:S(2)}, u32[]{:S(2)}) collective-permute-start(f32[224,896]{1,0:T(8,128)} %dynamic-slice_convert_fusion), channel_id=1, source_target_pairs={{0,1},{1,0},{2,3},{3,2},{4,5},{5,4},{6,7},{7,6},{8,9},{9,8},{10,11... | collective-permute-start | bytes 2408456 | tf_op jit(solution)/shard_map/ppermute | solution.py:59
  21.1 22.5 %collective-permute-start = (f32[512,448]{0,1:T(8,128)}, f32[512,448]{0,1:T(8,128)S(1)}, u32[]{:S(2)}, u32[]{:S(2)}) collective-permute-start(f32[512,448]{0,1:T(8,128)} %bitcast_convert_fusion), channel_id=1, source_target_pairs={{0,1},{1,0},{2,3},{3,2},{4,5},{5,4},{6,7},{7,6},{8,9},{9,8},{10,11... | collective-permute-start | bytes 2752520 | tf_op jit(solution)/shard_map/ppermute | solution.py:59
  24.4 6.3 %collective-permute-start.2 = (f32[224,896]{1,0:T(8,128)}, f32[224,896]{1,0:T(8,128)}, u32[]{:S(2)}, u32[]{:S(2)}) collective-permute-start(f32[224,896]{1,0:T(8,128)} %collective-permute-done.1), channel_id=1, source_target_pairs={{0,2},{2,0},{4,6},{6,4},{8,10},{10,8},{12,14},{14,12},{16,18},{18,... | collective-permute-start | bytes 2408456 | tf_op jit(solution)/shard_map/ppermute | solution.py:64
  26.2 52.9 %collective-permute-start.5 = (f32[512,896]{1,0:T(8,128)}, f32[512,896]{1,0:T(8,128)}, u32[]{:S(2)}, u32[]{:S(2)}) collective-permute-start(f32[512,896]{1,0:T(8,128)} %get-tuple-element.96), channel_id=1, source_target_pairs={{0,8},{2,10},{4,12},{6,14},{8,0},{10,2},{12,4},{14,6},{16,24},{18,... | collective-permute-start | bytes 5505032 | tf_op jit(solution)/shard_map/ppermute | solution.py:64
  46.3 62.2 %collective-permute-start.4 = (f32[512,896]{1,0:T(8,128)S(1)}, f32[512,896]{1,0:T(8,128)S(1)}, u32[]{:S(2)}, u32[]{:S(2)}) collective-permute-start(f32[512,896]{1,0:T(8,128)S(1)} %get-tuple-element.84), channel_id=1, source_target_pairs={{0,8},{2,10},{4,12},{6,14},{8,0},{10,2},{12,4},{14,6},{16,24},{18,... | collective-permute-start | bytes 5505032 | tf_op jit(solution)/shard_map/ppermute | solution.py:64
  134.4 20.1 %collective-permute-start.6 = (f32[224,2432]{1,0:T(8,128)}, f32[224,2432]{1,0:T(8,128)}, u32[]{:S(2)}, u32[]{:S(2)}) collective-permute-start(f32[224,2432]{1,0:T(8,128)} %fusion.60), channel_id=1, source_target_pairs={{0,2},{2,0},{4,6},{6,4},{8,10},{10,8},{12,14},{14,12},{16,18},{18,... | collective-permute-start | bytes 6537224 | tf_op jit(solution)/shard_map/ppermute | solution.py:64
  144.3 19.6 %collective-permute-start.7 = (f32[224,2432]{1,0:T(8,128)}, f32[224,2432]{1,0:T(8,128)}, u32[]{:S(2)}, u32[]{:S(2)}) collective-permute-start(f32[224,2432]{1,0:T(8,128)} %fusion.143), channel_id=1, source_target_pairs={{0,2},{2,0},{4,6},{6,4},{8,10},{10,8},{12,14},{14,12},{16,18},{18,... | collective-permute-start | bytes 6537224 | tf_op jit(solution)/shard_map/ppermute | solution.py:64
  148.1 20.9 %collective-permute-start.8 = (f32[224,2432]{1,0:T(8,128)}, f32[224,2432]{1,0:T(8,128)}, u32[]{:S(2)}, u32[]{:S(2)}) collective-permute-start(f32[224,2432]{1,0:T(8,128)} %fusion.144), channel_id=1, source_target_pairs={{0,2},{2,0},{4,6},{6,4},{8,10},{10,8},{12,14},{14,12},{16,18},{18,... | collective-permute-start | bytes 6537224 | tf_op jit(solution)/shard_map/ppermute | solution.py:64
  149.3 42.8 %collective-permute-start.3 = (f32[512,896]{1,0:T(8,128)S(1)}, f32[512,896]{1,0:T(8,128)S(1)}, u32[]{:S(2)}, u32[]{:S(2)}) collective-permute-start(f32[512,896]{1,0:T(8,128)S(1)} %get-tuple-element.32), channel_id=1, source_target_pairs={{0,1},{1,0},{2,3},{3,2},{4,5},{5,4},{6,7},{7,6},{8,9},{9,8},{10,11... | collective-permute-start | bytes 5505032 | tf_op jit(solution)/shard_map/ppermute | solution.py:59
  158.6 36.4 %collective-permute-start.28 = (f32[112,2432]{1,0:T(8,128)S(1)}, f32[112,2432]{1,0:T(8,128)S(1)}, u32[]{:S(2)}, u32[]{:S(2)}) collective-permute-start(f32[112,2432]{1,0:T(8,128)S(1)} %convolution_add_fusion.4), channel_id=1, source_target_pairs={{0,4},{2,6},{4,0},{6,2},{8,12},{10,14},{12,8},{14,10},{16,20},{18,... | collective-permute-start | bytes 3268616 | tf_op jit(solution)/shard_map/ppermute | solution.py:64
  166.2 68.0 %collective-permute-start.24 = (f32[112,2432]{1,0:T(8,128)S(1)}, f32[112,2432]{1,0:T(8,128)S(1)}, u32[]{:S(2)}, u32[]{:S(2)}) collective-permute-start(f32[112,2432]{1,0:T(8,128)S(1)} %convolution_add_fusion.2), channel_id=1, source_target_pairs={{0,4},{2,6},{4,0},{6,2},{8,12},{10,14},{12,8},{14,10},{16,20},{18,... | collective-permute-start | bytes 3268616 | tf_op jit(solution)/shard_map/ppermute | solution.py:64
  171.4 60.0 %collective-permute-start.26 = (f32[112,2432]{1,0:T(8,128)S(1)}, f32[112,2432]{1,0:T(8,128)S(1)}, u32[]{:S(2)}, u32[]{:S(2)}) collective-permute-start(f32[112,2432]{1,0:T(8,128)S(1)} %convolution_add_fusion), channel_id=1, source_target_pairs={{0,4},{2,6},{4,0},{6,2},{8,12},{10,14},{12,8},{14,10},{16,20},{18,... | collective-permute-start | bytes 3268616 | tf_op jit(solution)/shard_map/ppermute | solution.py:64
  193.2 88.8 %collective-permute-start.9 = (f32[512,896]{1,0:T(8,128)S(1)}, f32[512,896]{1,0:T(8,128)S(1)}, u32[]{:S(2)}, u32[]{:S(2)}) collective-permute-start(f32[512,896]{1,0:T(8,128)S(1)} %copy-done.9), channel_id=1, source_target_pairs={{0,1},{1,0},{2,3},{3,2},{4,5},{5,4},{6,7},{7,6},{8,9},{9,8},{10,11... | collective-permute-start | bytes 5505032 | tf_op jit(solution)/shard_map/ppermute | solution.py:59
  195.1 39.6 %collective-permute-start.29 = (f32[56,2432]{1,0:T(8,128)S(1)}, f32[56,2432]{1,0:T(8,128)S(1)}, u32[]{:S(2)}, u32[]{:S(2)}) collective-permute-start(f32[56,2432]{1,0:T(8,128)S(1)} %slice_add_fusion), channel_id=1, source_target_pairs={{0,16},{2,18},{4,20},{6,22},{8,24},{10,26},{12,28},{14,30},{16,0},... | collective-permute-start | bytes 1634312 | tf_op jit(solution)/shard_map/ppermute | solution.py:64
  231.5 39.0 %collective-permute-start.27 = (f32[56,2432]{1,0:T(8,128)S(1)}, f32[56,2432]{1,0:T(8,128)S(1)}, u32[]{:S(2)}, u32[]{:S(2)}) collective-permute-start(f32[56,2432]{1,0:T(8,128)S(1)} %slice_add_fusion.2), channel_id=1, source_target_pairs={{0,16},{2,18},{4,20},{6,22},{8,24},{10,26},{12,28},{14,30},{16,0},... | collective-permute-start | bytes 1634312 | tf_op jit(solution)/shard_map/ppermute | solution.py:64
  234.3 46.9 %collective-permute-start.25 = (f32[56,2432]{1,0:T(8,128)S(1)}, f32[56,2432]{1,0:T(8,128)S(1)}, u32[]{:S(2)}, u32[]{:S(2)}) collective-permute-start(f32[56,2432]{1,0:T(8,128)S(1)} %slice_add_fusion.4), channel_id=1, source_target_pairs={{0,16},{2,18},{4,20},{6,22},{8,24},{10,26},{12,28},{14,30},{16,0},... | collective-permute-start | bytes 1634312 | tf_op jit(solution)/shard_map/ppermute | solution.py:64
  302.3 11.7 %collective-permute-start.20 = (f32[448,448]{1,0:T(8,128)}, f32[448,448]{1,0:T(8,128)}, u32[]{:S(2)}, u32[]{:S(2)}) collective-permute-start(f32[448,448]{1,0:T(8,128)} %fusion.49), channel_id=1, source_target_pairs={{0,2},{2,0},{4,6},{6,4},{8,10},{10,8},{12,14},{14,12},{16,18},{18,... | collective-permute-start | bytes 2408456 | tf_op jit(solution)/shard_map/ppermute | solution.py:64
  307.2 10.2 %collective-permute-start.11 = (f32[448,576]{1,0:T(8,128)}, f32[448,576]{1,0:T(8,128)}, u32[]{:S(2)}, u32[]{:S(2)}) collective-permute-start(f32[448,576]{1,0:T(8,128)} %fusion.52), channel_id=1, source_target_pairs={{0,2},{2,0},{4,6},{6,4},{8,10},{10,8},{12,14},{14,12},{16,18},{18,... | collective-permute-start | bytes 3096584 | tf_op jit(solution)/shard_map/ppermute | solution.py:64
  311.3 42.3 %collective-permute-start.10 = (f32[512,896]{1,0:T(8,128)}, f32[512,896]{1,0:T(8,128)}, u32[]{:S(2)}, u32[]{:S(2)}) collective-permute-start(f32[512,896]{1,0:T(8,128)} %fusion.145), channel_id=1, source_target_pairs={{0,1},{1,0},{2,3},{3,2},{4,5},{5,4},{6,7},{7,6},{8,9},{9,8},{10,11... | collective-permute-start | bytes 5505032 | tf_op jit(solution)/shard_map/ppermute | solution.py:59
  315.4 13.5 %collective-permute-start.21 = (f32[224,448]{1,0:T(8,128)S(1)}, f32[224,448]{1,0:T(8,128)S(1)}, u32[]{:S(2)}, u32[]{:S(2)}) collective-permute-start(f32[224,448]{1,0:T(8,128)S(1)} %convolution_add_fusion.9), channel_id=1, source_target_pairs={{0,8},{2,10},{4,12},{6,14},{8,0},{10,2},{12,4},{14,6},{16,24},{18,... | collective-permute-start | bytes 1204232 | tf_op jit(solution)/shard_map/ppermute | solution.py:64
  318.9 38.3 %collective-permute-start.12 = (f32[224,576]{1,0:T(8,128)S(1)}, f32[224,576]{1,0:T(8,128)S(1)}, u32[]{:S(2)}, u32[]{:S(2)}) collective-permute-start(f32[224,576]{1,0:T(8,128)S(1)} %convolution_add_fusion.7), channel_id=1, source_target_pairs={{0,8},{2,10},{4,12},{6,14},{8,0},{10,2},{12,4},{14,6},{16,24},{18,... | collective-permute-start | bytes 1548296 | tf_op jit(solution)/shard_map/ppermute | solution.py:64
  335.1 25.2 %collective-permute-start.23 = (f32[56,448]{1,0:T(8,128)S(1)}, f32[56,448]{1,0:T(8,128)S(1)}, u32[]{:S(2)}, u32[]{:S(2)}) collective-permute-start(f32[56,448]{1,0:T(8,128)S(1)} %slice_add_fusion.12), channel_id=1, source_target_pairs={{0,16},{2,18},{4,20},{6,22},{8,24},{10,26},{12,28},{14,30},{16,0},... | collective-permute-start | bytes 301064 | tf_op jit(solution)/shard_map/ppermute | solution.py:64
  357.2 7.8 %collective-permute-start.13 = (f32[112,576]{1,0:T(8,128)S(1)}, f32[112,576]{1,0:T(8,128)S(1)}, u32[]{:S(2)}, u32[]{:S(2)}) collective-permute-start(f32[112,576]{1,0:T(8,128)S(1)} %get-tuple-element.95), channel_id=1, source_target_pairs={{0,4},{2,6},{4,0},{6,2},{8,12},{10,14},{12,8},{14,10},{16,20},{18,... | collective-permute-start | bytes 774152 | tf_op jit(solution)/shard_map/ppermute | solution.py:64
  365.7 13.8 %collective-permute-start.14 = (f32[56,576]{1,0:T(8,128)}, f32[56,576]{1,0:T(8,128)S(1)}, u32[]{:S(2)}, u32[]{:S(2)}) collective-permute-start(f32[56,576]{1,0:T(8,128)} %slice_add_fusion.10), channel_id=1, source_target_pairs={{0,16},{2,18},{4,20},{6,22},{8,24},{10,26},{12,28},{14,30},{16,0},... | collective-permute-start | bytes 387080 | tf_op jit(solution)/shard_map/ppermute | solution.py:64
  (77 other events, 762.2 us)
